TPU v7x, 32 devices: a whole 2x2x4 slice. The times are simulated.
32 devices in a mesh: cube: 16 (over z, y, x), front: 2 (over core).
Axes of the slice: x: 2, y: 2, z: 4, core: 2. Of those that a mesh axis runs over, the one named last changes fastest.
Arguments:
- elem_loads: float32 [64, 8192], P(None, ('cube', 'front')), may hold values from -6 to 6
- elem_owner: int32 [8192, 1], P(('cube', 'front')), may hold values from 0 to 31; in each aligned block of 256 rows (0 to 255, 256 to 511, ...) at most 16 rows name the same one
- elem_row: int32 [8192], P(('cube', 'front')), may hold values from 0 to 1023
- sep_loads: float32 [4, 64, 512], P(None, None, ('cube', 'front')), may hold values from -6 to 6
- leaf_inverse: float32 [32768, 1024], P(('cube', 'front'))
- leaf_coupling: float32 [64, 32768], P(None, ('cube', 'front')), may hold values from -0.09375 to 0.09375
- coupling0: float32 [512, 512], P(None, ('cube', 'front')), may hold values from -0.25 to 0.25
- coupling1: float32 [256, 512], P(None, ('cube', 'front')), may hold values from -0.375 to 0.375
- coupling2: float32 [128, 512], P(None, ('cube', 'front')), may hold values from -0.5 to 0.5
- inverse0: float32 [512, 512], P(('cube', 'front'))
- inverse1: float32 [512, 256], P(('cube', 'front'))
- inverse2: float32 [512, 128], P(('cube', 'front'))
- inverse3: float32 [512, 64], P(('cube', 'front'))
Outputs:
- leaf_solution: float32 [64, 32768], P(None, ('cube', 'front'))
- sep_solution: float32 [4, 64, 512], P(None, None, ('cube', 'front'))
Inputs may be any that keep to these rules, and one draw needn't show every extreme that they name: `elem_owner`: among the element rows of one device, at most 16 name the same owner, a bound that some block reaches.
All inputs are finite; a program needn't handle non-finite values.
Results may differ from a plain program's by a relative error of at most 0.00012.
Values sent between devices are 32-bit elements; how exact they have to be, the bound alone decides.
A program may use at most 64 MiB of HBM per device.

v0:
```python
import jax
import jax.numpy as jnp
from jax import lax
from jax.sharding import PartitionSpec as P

HIGH = lax.Precision.HIGHEST


def partner(block, axis, apart):
    count = lax.axis_size(axis)
    route = []
    for low in range(count):
        high = low | 1 << apart
        if high != low and high < count:
            route += [(low, high), (high, low)]
    return lax.ppermute(block, axis, route)


def row_dot(left, right):
    return lax.dot_general(left, right, (((1,), (1,)), ((), ())), precision=HIGH)


def mat_dot(left, right):
    return jnp.dot(left, right, precision=HIGH)


def reduce_rows(term, group, position):
    current = term
    for bit in reversed(range(group.bit_length() - 1)):
        half = current.shape[1] // 2
        lower, upper = (current[:, :half], current[:, half:])
        mine = position >> bit & 1 == 1
        keep = jnp.where(mine, upper, lower)
        leave = jnp.where(mine, lower, upper)
        current = keep + partner(leave, ("cube", "front"), bit)
    return current


def gather_rows(local, group, position):
    current = local
    for bit in range(group.bit_length() - 1):
        other = partner(current, ("cube", "front"), bit)
        mine = position >> bit & 1 == 1
        current = jnp.where(
            mine, jnp.concatenate([other, current], 1), jnp.concatenate([current, other], 1)
        )
    return current


def total_rows(term, group):
    current = term
    for bit in range(group.bit_length() - 1):
        current = current + partner(current, ("cube", "front"), bit)
    return current


def shards(
    elem_loads,
    elem_owner,
    elem_row,
    sep_loads,
    leaf_inverse,
    leaf_coupling,
    coupling0,
    coupling1,
    coupling2,
    inverse0,
    inverse1,
    inverse2,
    inverse3,
):
    position = lax.axis_index(("cube", "front"))
    devices = lax.axis_size(("cube", "front"))
    columns = elem_loads.shape[0]
    leaf_rows = leaf_inverse.shape[0]
    sep_rows = sep_loads.shape[2]
    count = elem_owner.shape[0]
    capacity = 2 * count // devices
    owner = elem_owner[:, 0]
    marks = (owner[:, None] == jnp.arange(devices, dtype=jnp.int32)[None, :]).astype(jnp.int32)
    ranks = jnp.sum(jnp.cumsum(marks, axis=0) * marks, axis=1) - 1
    slots = owner * capacity + ranks
    send_vals = jnp.zeros((columns, devices * capacity), jnp.float32).at[:, slots].set(elem_loads)
    send_rows = jnp.full((1, devices * capacity), -1, jnp.int32).at[0, slots].set(elem_row)
    got_vals, got_rows = (
        lax.all_to_all(send_vals, ("cube", "front"), split_axis=1, concat_axis=1, tiled=True),
        lax.all_to_all(send_rows, ("cube", "front"), split_axis=1, concat_axis=1, tiled=True),
    )
    placing = (got_rows[0][:, None] == jnp.arange(leaf_rows, dtype=jnp.int32)[None, :]).astype(
        jnp.float32
    )
    loads = mat_dot(got_vals, placing)
    leaf_y = row_dot(loads, leaf_inverse)
    inverses = [inverse0, inverse1, inverse2, inverse3]
    couplings = [coupling0, coupling1, coupling2, leaf_coupling]
    sep_y = [None] * 4
    child = leaf_y
    for level in (3, 2, 1, 0):
        group = devices >> level
        term = row_dot(child, couplings[level])
        resid = sep_loads[level] - reduce_rows(term, group, position)
        sep_y[level] = row_dot(gather_rows(resid, group, position), inverses[level])
        child = sep_y[level]
    solved = []
    parent = None
    for level in range(4):
        group = devices >> level
        upper = sep_y[level]
        if level > 0:
            upper = upper - mat_dot(parent, couplings[level - 1])
        term = mat_dot(upper, inverses[level])
        parent = total_rows(term, group)
        mine = lax.dynamic_slice_in_dim(parent, position % group * sep_rows, sep_rows, 1)
        solved.append(mine)
    upper = leaf_y - mat_dot(parent, leaf_coupling)
    leaf_solution = mat_dot(upper, leaf_inverse)
    return (leaf_solution, jnp.stack(solved))


def solution(mesh):
    in_specs = (
        P(None, ("cube", "front")),
        P(("cube", "front"), None),
        P(("cube", "front")),
        P(None, None, ("cube", "front")),
        P(("cube", "front"), None),
        P(None, ("cube", "front")),
        P(None, ("cube", "front")),
        P(None, ("cube", "front")),
        P(None, ("cube", "front")),
        P(("cube", "front"), None),
        P(("cube", "front"), None),
        P(("cube", "front"), None),
        P(("cube", "front"), None),
    )
    out_specs = (P(None, ("cube", "front")), P(None, None, ("cube", "front")))
    return jax.shard_map(shards, mesh=mesh, in_specs=in_specs, out_specs=out_specs, check_vma=False)
```

profile of v0, /device:TPU:0, one launch (start us, length us, event | category | flops | bytes accessed | tf_op | source)
XLA Modules:
  0.0 199.2 jit_solution(2309752474257731399)
XLA Ops:
  0.7 0.7 fusion.32
  2.2 0.8 fusion.25
  3.7 1.6 scatter_custom_fusion.1
  5.9 7.3 %all-to-all-start.1 = ((s32[1,32,16]{2,0,1:T(1,128)}), s32[1,32,16]{2,0,1:T(1,128)S(1)}, u32[]{:S(2)}, u32[]{:S(2)}) async-start(s32[1,32,16]{2,0,1:T(1,128)} %bitcast.8), calls=%async_computation.1 | async-start | bytes 32768 | tf_op jit(solution)/shard_map/all_to_all | solution.py:87
  13.3 0.9 copy.34
  14.2 1.2 scatter_custom_fusion
  15.4 0.8 reshape.69
  16.3 4.1 %all-to-all-done.1 = s32[1,32,16]{2,0,1:T(1,128)S(1)} async-done(((s32[1,32,16]{2,0,1:T(1,128)}), s32[1,32,16]{2,0,1:T(1,128)S(1)}, u32[]{:S(2)}, u32[]{:S(2)}) %all-to-all-start.1) | async-done | bytes 2080 | tf_op jit(solution)/shard_map/all_to_all | solution.py:87
  20.4 2.8 %all-to-all-start = ((f32[32,1,1024]{2,1,0:T(1,128)}), f32[32,1,1024]{2,1,0:T(1,128)S(1)}, u32[]{:S(2)}, u32[]{:S(2)}) async-start(f32[32,1,1024]{2,1,0:T(1,128)} %reshape.69), calls=%async_computation | async-start | bytes 262144 | tf_op jit(solution)/shard_map/all_to_all | solution.py:86
  24.4 6.7 %all-to-all-done = f32[32,1,1024]{2,1,0:T(1,128)S(1)} async-done(((f32[32,1,1024]{2,1,0:T(1,128)}), f32[32,1,1024]{2,1,0:T(1,128)S(1)}, u32[]{:S(2)}, u32[]{:S(2)}) %all-to-all-start) | async-done | bytes 131104 | tf_op jit(solution)/shard_map/all_to_all | solution.py:86
  31.7 0.9 reduce.6
  32.7 1.0 fusion
  33.7 6.3 %fusion.41 = f32[64,1024]{1,0:T(8,128)S(1)} fusion(f32[64,1024]{1,0:T(8,128)S(1)} %fusion, f32[1024,1024]{1,0:T(8,128)} %param.17), kind=kOutput, calls=%fused_computation.102 | convolution fusion | flops 805306368 | bytes 4718592 | tf_op jit(solution)/shard_map/dot_general | solution.py:20
  40.8 3.4 %collective-permute-done = f32[64,32]{0,1:T(8,128)S(1)} collective-permute-done((f32[64,32]{0,1:T(8,128)S(1)}, f32[64,32]{0,1:T(8,128)S(1)}, u32[]{:S(2)}, u32[]{:S(2)}) %collective-permute-start) | collective-permute-done | bytes 8224 | tf_op jit(solution)/shard_map/ppermute | solution.py:16
  44.3 1.2 collective-permute-done.1
  45.6 1.1 collective-permute-done.2
  47.0 3.4 %collective-permute-done.3 = f32[64,32]{0,1:T(8,128)S(1)} collective-permute-done((f32[64,32]{0,1:T(8,128)S(1)}, f32[64,32]{0,1:T(8,128)S(1)}, u32[]{:S(2)}, u32[]{:S(2)}) %collective-permute-start.3) | collective-permute-done | bytes 8224 | tf_op jit(solution)/shard_map/ppermute | solution.py:16
  50.9 0.7 collective-permute-start.4
  51.6 3.3 %collective-permute-done.4 = f32[64,64]{0,1:T(8,128)S(1)} collective-permute-done((f32[64,64]{0,1:T(8,128)S(1)}, f32[64,64]{0,1:T(8,128)S(1)}, u32[]{:S(2)}, u32[]{:S(2)}) %collective-permute-start.4) | collective-permute-done | bytes 16416 | tf_op jit(solution)/shard_map/ppermute | solution.py:16
  55.3 3.4 %collective-permute-done.5 = f32[64,32]{0,1:T(8,128)S(1)} collective-permute-done((f32[64,32]{0,1:T(8,128)S(1)}, f32[64,32]{0,1:T(8,128)S(1)}, u32[]{:S(2)}, u32[]{:S(2)}) %collective-permute-start.5) | collective-permute-done | bytes 8224 | tf_op jit(solution)/shard_map/ppermute | solution.py:16
  58.8 1.2 collective-permute-done.6
  60.1 1.0 collective-permute-done.7
  61.5 3.4 %collective-permute-done.8 = f32[64,32]{0,1:T(8,128)S(1)} collective-permute-done((f32[64,32]{0,1:T(8,128)S(1)}, f32[64,32]{0,1:T(8,128)S(1)}, u32[]{:S(2)}, u32[]{:S(2)}) %collective-permute-start.8) | collective-permute-done | bytes 8224 | tf_op jit(solution)/shard_map/ppermute | solution.py:16
  65.5 3.3 %collective-permute-done.9 = f32[64,64]{0,1:T(8,128)S(1)} collective-permute-done((f32[64,64]{0,1:T(8,128)S(1)}, f32[64,64]{0,1:T(8,128)S(1)}, u32[]{:S(2)}, u32[]{:S(2)}) %collective-permute-start.9) | collective-permute-done | bytes 16416 | tf_op jit(solution)/shard_map/ppermute | solution.py:16
  69.4 0.7 collective-permute-start.10
  70.1 3.6 %collective-permute-done.10 = f32[64,128]{0,1:T(8,128)S(1)} collective-permute-done((f32[64,128]{0,1:T(8,128)S(1)}, f32[64,128]{0,1:T(8,128)S(1)}, u32[]{:S(2)}, u32[]{:S(2)}) %collective-permute-start.10) | collective-permute-done | bytes 32800 | tf_op jit(solution)/shard_map/ppermute | solution.py:16
  73.8 0.7 collective-permute-start.11
  74.5 3.3 %collective-permute-done.11 = f32[64,64]{0,1:T(8,128)S(1)} collective-permute-done((f32[64,64]{0,1:T(8,128)S(1)}, f32[64,64]{0,1:T(8,128)S(1)}, u32[]{:S(2)}, u32[]{:S(2)}) %collective-permute-start.11) | collective-permute-done | bytes 16416 | tf_op jit(solution)/shard_map/ppermute | solution.py:16
  78.2 3.4 %collective-permute-done.12 = f32[64,32]{0,1:T(8,128)S(1)} collective-permute-done((f32[64,32]{0,1:T(8,128)S(1)}, f32[64,32]{0,1:T(8,128)S(1)}, u32[]{:S(2)}, u32[]{:S(2)}) %collective-permute-start.12) | collective-permute-done | bytes 8224 | tf_op jit(solution)/shard_map/ppermute | solution.py:16
  81.6 1.2 collective-permute-done.13
  83.0 1.0 collective-permute-done.14
  84.3 3.4 %collective-permute-done.15 = f32[64,32]{0,1:T(8,128)S(1)} collective-permute-done((f32[64,32]{0,1:T(8,128)S(1)}, f32[64,32]{0,1:T(8,128)S(1)}, u32[]{:S(2)}, u32[]{:S(2)}) %collective-permute-start.15) | collective-permute-done | bytes 8224 | tf_op jit(solution)/shard_map/ppermute | solution.py:16
  88.4 3.3 %collective-permute-done.16 = f32[64,64]{0,1:T(8,128)S(1)} collective-permute-done((f32[64,64]{0,1:T(8,128)S(1)}, f32[64,64]{0,1:T(8,128)S(1)}, u32[]{:S(2)}, u32[]{:S(2)}) %collective-permute-start.16) | collective-permute-done | bytes 16416 | tf_op jit(solution)/shard_map/ppermute | solution.py:16
  91.7 0.7 collective-permute-start.17
  92.4 3.6 %collective-permute-done.17 = f32[64,128]{0,1:T(8,128)S(1)} collective-permute-done((f32[64,128]{0,1:T(8,128)S(1)}, f32[64,128]{0,1:T(8,128)S(1)}, u32[]{:S(2)}, u32[]{:S(2)}) %collective-permute-start.17) | collective-permute-done | bytes 32800 | tf_op jit(solution)/shard_map/ppermute | solution.py:16
  96.8 0.8 collective-permute-start.18
  97.7 6.5 %collective-permute-done.18 = f32[64,256]{0,1:T(8,128)S(1)} collective-permute-done((f32[64,256]{0,1:T(8,128)S(1)}, f32[64,256]{0,1:T(8,128)S(1)}, u32[]{:S(2)}, u32[]{:S(2)}) %collective-permute-start.18) | collective-permute-done | bytes 65568 | tf_op jit(solution)/shard_map/ppermute | solution.py:16
  104.3 4.3 %collective-permute-done.19 = f32[64,128]{0,1:T(8,128)S(1)} collective-permute-done((f32[64,128]{0,1:T(8,128)S(1)}, f32[64,128]{0,1:T(8,128)S(1)}, u32[]{:S(2)}, u32[]{:S(2)}) %collective-permute-start.19) | collective-permute-done | bytes 32800 | tf_op jit(solution)/shard_map/ppermute | solution.py:16
  108.6 0.7 collective-permute-start.20
  109.3 3.3 %collective-permute-done.20 = f32[64,64]{0,1:T(8,128)S(1)} collective-permute-done((f32[64,64]{0,1:T(8,128)S(1)}, f32[64,64]{0,1:T(8,128)S(1)}, u32[]{:S(2)}, u32[]{:S(2)}) %collective-permute-start.20) | collective-permute-done | bytes 16416 | tf_op jit(solution)/shard_map/ppermute | solution.py:16
  113.1 3.4 %collective-permute-done.21 = f32[64,32]{0,1:T(8,128)S(1)} collective-permute-done((f32[64,32]{0,1:T(8,128)S(1)}, f32[64,32]{0,1:T(8,128)S(1)}, u32[]{:S(2)}, u32[]{:S(2)}) %collective-permute-start.21) | collective-permute-done | bytes 8224 | tf_op jit(solution)/shard_map/ppermute | solution.py:16
  116.5 1.2 collective-permute-done.22
  117.8 1.0 collective-permute-done.23
  119.2 3.4 %collective-permute-done.24 = f32[64,32]{0,1:T(8,128)S(1)} collective-permute-done((f32[64,32]{0,1:T(8,128)S(1)}, f32[64,32]{0,1:T(8,128)S(1)}, u32[]{:S(2)}, u32[]{:S(2)}) %collective-permute-start.24) | collective-permute-done | bytes 8224 | tf_op jit(solution)/shard_map/ppermute | solution.py:16
  123.2 3.3 %collective-permute-done.25 = f32[64,64]{0,1:T(8,128)S(1)} collective-permute-done((f32[64,64]{0,1:T(8,128)S(1)}, f32[64,64]{0,1:T(8,128)S(1)}, u32[]{:S(2)}, u32[]{:S(2)}) %collective-permute-start.25) | collective-permute-done | bytes 16416 | tf_op jit(solution)/shard_map/ppermute | solution.py:16
  126.6 4.3 %collective-permute-done.26 = f32[64,128]{0,1:T(8,128)S(1)} collective-permute-done((f32[64,128]{0,1:T(8,128)S(1)}, f32[64,128]{0,1:T(8,128)S(1)}, u32[]{:S(2)}, u32[]{:S(2)}) %collective-permute-start.26) | collective-permute-done | bytes 32800 | tf_op jit(solution)/shard_map/ppermute | solution.py:16
  131.0 7.0 %collective-permute-done.27 = f32[64,256]{0,1:T(8,128)S(1)} collective-permute-done((f32[64,256]{0,1:T(8,128)S(1)}, f32[64,256]{0,1:T(8,128)S(1)}, u32[]{:S(2)}, u32[]{:S(2)}) %collective-permute-start.27) | collective-permute-done | bytes 65568 | tf_op jit(solution)/shard_map/ppermute | solution.py:16
  138.7 1.3 collective-permute-done.28
  140.5 5.2 %collective-permute-done.29 = f32[64,512]{1,0:T(8,128)S(1)} collective-permute-done((f32[64,512]{1,0:T(8,128)S(1)}, f32[64,512]{1,0:T(8,128)S(1)}, u32[]{:S(2)}, u32[]{:S(2)}) %collective-permute-start.29) | collective-permute-done | bytes 131104 | tf_op jit(solution)/shard_map/ppermute | solution.py:16
  145.7 0.7 collective-permute-start.30
  146.4 4.3 %collective-permute-done.30 = f32[64,512]{1,0:T(8,128)S(1)} collective-permute-done((f32[64,512]{1,0:T(8,128)S(1)}, f32[64,512]{1,0:T(8,128)S(1)}, u32[]{:S(2)}, u32[]{:S(2)}) %collective-permute-start.30) | collective-permute-done | bytes 131104 | tf_op jit(solution)/shard_map/ppermute | solution.py:16
  150.8 5.0 %collective-permute-done.31 = f32[64,512]{1,0:T(8,128)S(1)} collective-permute-done((f32[64,512]{1,0:T(8,128)S(1)}, f32[64,512]{1,0:T(8,128)S(1)}, u32[]{:S(2)}, u32[]{:S(2)}) %collective-permute-start.31) | collective-permute-done | bytes 131104 | tf_op jit(solution)/shard_map/ppermute | solution.py:16
  155.9 6.7 %collective-permute-done.32 = f32[64,512]{1,0:T(8,128)S(1)} collective-permute-done((f32[64,512]{1,0:T(8,128)S(1)}, f32[64,512]{1,0:T(8,128)S(1)}, u32[]{:S(2)}, u32[]{:S(2)}) %collective-permute-start.32) | collective-permute-done | bytes 131104 | tf_op jit(solution)/shard_map/ppermute | solution.py:16
  163.2 1.2 collective-permute-done.33
  164.9 3.9 %collective-permute-done.34 = f32[64,256]{1,0:T(8,128)S(1)} collective-permute-done((f32[64,256]{1,0:T(8,128)S(1)}, f32[64,256]{1,0:T(8,128)S(1)}, u32[]{:S(2)}, u32[]{:S(2)}) %collective-permute-start.34) | collective-permute-done | bytes 65568 | tf_op jit(solution)/shard_map/ppermute | solution.py:16
  168.8 0.7 collective-permute-start.35
  169.5 3.6 %collective-permute-done.35 = f32[64,256]{1,0:T(8,128)S(1)} collective-permute-done((f32[64,256]{1,0:T(8,128)S(1)}, f32[64,256]{1,0:T(8,128)S(1)}, u32[]{:S(2)}, u32[]{:S(2)}) %collective-permute-start.35) | collective-permute-done | bytes 65568 | tf_op jit(solution)/shard_map/ppermute | solution.py:16
  173.2 4.3 %collective-permute-done.36 = f32[64,256]{1,0:T(8,128)S(1)} collective-permute-done((f32[64,256]{1,0:T(8,128)S(1)}, f32[64,256]{1,0:T(8,128)S(1)}, u32[]{:S(2)}, u32[]{:S(2)}) %collective-permute-start.36) | collective-permute-done | bytes 65568 | tf_op jit(solution)/shard_map/ppermute | solution.py:16
  178.0 1.2 collective-permute-done.37
  179.6 3.5 %collective-permute-done.38 = f32[64,128]{1,0:T(8,128)S(1)} collective-permute-done((f32[64,128]{1,0:T(8,128)S(1)}, f32[64,128]{1,0:T(8,128)S(1)}, u32[]{:S(2)}, u32[]{:S(2)}) %collective-permute-start.38) | collective-permute-done | bytes 32800 | tf_op jit(solution)/shard_map/ppermute | solution.py:16
  183.9 3.1 %collective-permute-done.39 = f32[64,128]{1,0:T(8,128)S(1)} collective-permute-done((f32[64,128]{1,0:T(8,128)S(1)}, f32[64,128]{1,0:T(8,128)S(1)}, u32[]{:S(2)}, u32[]{:S(2)}) %collective-permute-start.39) | collective-permute-done | bytes 32800 | tf_op jit(solution)/shard_map/ppermute | solution.py:16
  187.7 1.0 collective-permute-done.40
  189.2 3.4 %collective-permute-done.41 = f32[64,64]{0,1:T(8,128)S(1)} collective-permute-done((f32[64,64]{0,1:T(8,128)S(1)}, f32[64,64]{0,1:T(8,128)S(1)}, u32[]{:S(2)}, u32[]{:S(2)}) %collective-permute-start.41) | collective-permute-done | bytes 16416 | tf_op jit(solution)/shard_map/ppermute | solution.py:16
  193.1 5.5 %fusion.50 = f32[64,1024]{1,0:T(8,128)} fusion(f32[64,1024]{1,0:T(8,128)S(1)} %convolution_subtract_fusion, f32[1024,1024]{1,0:T(8,128)} %param.17), kind=kOutput, calls=%fused_computation.111 | convolution fusion | flops 805306368 | bytes 4718592 | tf_op jit(solution)/shard_map/dot_general | solution.py:24
  (140 shorter events, 19.1 us)
Async XLA Ops:
  0.6 39.4 %copy-start = (f32[64,1024]{1,0:T(8,128)S(1)}, f32[64,1024]{1,0:T(8,128)}, u32[]{:S(2)}) copy-start(f32[64,1024]{1,0:T(8,128)} %param.18) | copy-start | bytes 786436
  0.6 44.8 %copy-start.4 = (f32[4,64,16]{1,2,0:T(8,128)S(1)}, f32[4,64,16]{1,2,0:T(8,128)}, u32[]{:S(2)}) copy-start(f32[4,64,16]{1,2,0:T(8,128)} %param.16) | copy-start | bytes 49156
  0.7 49.8 %copy-start.8 = (f32[16,64]{1,0:T(8,128)S(1)}, f32[16,64]{1,0:T(8,128)}, u32[]{:S(2)}) copy-start(f32[16,64]{1,0:T(8,128)} %param.25) | copy-start | bytes 12292
  0.7 49.9 %copy-start.3 = (f32[128,16]{0,1:T(8,128)S(1)}, f32[128,16]{0,1:T(8,128)}, u32[]{:S(2)}) copy-start(f32[128,16]{0,1:T(8,128)} %param.21) | copy-start | bytes 24580
  5.9 14.4 %all-to-all-start.1 = ((s32[1,32,16]{2,0,1:T(1,128)}), s32[1,32,16]{2,0,1:T(1,128)S(1)}, u32[]{:S(2)}, u32[]{:S(2)}) async-start(s32[1,32,16]{2,0,1:T(1,128)} %bitcast.8), calls=%async_computation.1 | async-start | bytes 32768 | tf_op jit(solution)/shard_map/all_to_all | solution.py:87
  14.2 54.6 %copy-start.7 = (f32[16,128]{1,0:T(8,128)S(1)}, f32[16,128]{1,0:T(8,128)}, u32[]{:S(2)}) copy-start(f32[16,128]{1,0:T(8,128)} %param.24) | copy-start | bytes 24580
  15.4 53.5 %copy-start.2 = (f32[256,16]{0,1:T(8,128)S(1)}, f32[256,16]{0,1:T(8,128)}, u32[]{:S(2)}) copy-start(f32[256,16]{0,1:T(8,128)} %param.20) | copy-start | bytes 49156
  20.4 10.8 %all-to-all-start = ((f32[32,1,1024]{2,1,0:T(1,128)}), f32[32,1,1024]{2,1,0:T(1,128)S(1)}, u32[]{:S(2)}, u32[]{:S(2)}) async-start(f32[32,1,1024]{2,1,0:T(1,128)} %reshape.69), calls=%async_computation | async-start | bytes 262144 | tf_op jit(solution)/shard_map/all_to_all | solution.py:86
  32.6 63.4 %copy-start.6 = (f32[16,256]{1,0:T(8,128)S(1)}, f32[16,256]{1,0:T(8,128)}, u32[]{:S(2)}) copy-start(f32[16,256]{1,0:T(8,128)} %param.23) | copy-start | bytes 49156
  32.7 63.5 %copy-start.1 = (f32[512,16]{0,1:T(8,128)S(1)}, f32[512,16]{0,1:T(8,128)}, u32[]{:S(2)}) copy-start(f32[512,16]{0,1:T(8,128)} %param.19) | copy-start | bytes 98308
  33.7 104.3 %copy-start.5 = (f32[16,512]{1,0:T(8,128)S(1)}, f32[16,512]{1,0:T(8,128)}, u32[]{:S(2)}) copy-start(f32[16,512]{1,0:T(8,128)} %param.22) | copy-start | bytes 98308
  40.4 3.8 %collective-permute-start = (f32[64,32]{0,1:T(8,128)S(1)}, f32[64,32]{0,1:T(8,128)S(1)}, u32[]{:S(2)}, u32[]{:S(2)}) collective-permute-start(f32[64,32]{0,1:T(8,128)S(1)} %slice_select_fusion.9), channel_id=1, source_target_pairs={{0,2},{2,0},{1,3},{3,1},{4,6},{6,4},{5,7},{7,5},{8,10},{10,8},{9,1... | collective-permute-start | bytes 24584 | tf_op jit(solution)/shard_map/ppermute | solution.py:16
  44.2 1.2 collective-permute-start.1
  45.4 1.2 collective-permute-start.2
  46.7 3.7 %collective-permute-start.3 = (f32[64,32]{0,1:T(8,128)S(1)}, f32[64,32]{0,1:T(8,128)S(1)}, u32[]{:S(2)}, u32[]{:S(2)}) collective-permute-start(f32[64,32]{0,1:T(8,128)S(1)} %maximum_select_fusion.14), channel_id=1, source_target_pairs={{0,2},{2,0},{1,3},{3,1},{4,6},{6,4},{5,7},{7,5},{8,10},{10,8},{9,1... | collective-permute-start | bytes 24584 | tf_op jit(solution)/shard_map/ppermute | solution.py:16
  50.9 4.0 %collective-permute-start.4 = (f32[64,64]{0,1:T(8,128)S(1)}, f32[64,64]{0,1:T(8,128)S(1)}, u32[]{:S(2)}, u32[]{:S(2)}) collective-permute-start(f32[64,64]{0,1:T(8,128)S(1)} %slice_select_fusion.5), channel_id=1, source_target_pairs={{0,4},{4,0},{1,5},{5,1},{2,6},{6,2},{3,7},{7,3},{8,12},{12,8},{9,1... | collective-permute-start | bytes 49160 | tf_op jit(solution)/shard_map/ppermute | solution.py:16
  54.9 3.8 %collective-permute-start.5 = (f32[64,32]{0,1:T(8,128)S(1)}, f32[64,32]{0,1:T(8,128)S(1)}, u32[]{:S(2)}, u32[]{:S(2)}) collective-permute-start(f32[64,32]{0,1:T(8,128)S(1)} %slice_select_fusion.8), channel_id=1, source_target_pairs={{0,2},{2,0},{1,3},{3,1},{4,6},{6,4},{5,7},{7,5},{8,10},{10,8},{9,1... | collective-permute-start | bytes 24584 | tf_op jit(solution)/shard_map/ppermute | solution.py:16
  58.7 1.2 collective-permute-start.6
  60.0 1.2 collective-permute-start.7
  61.1 3.7 %collective-permute-start.8 = (f32[64,32]{0,1:T(8,128)S(1)}, f32[64,32]{0,1:T(8,128)S(1)}, u32[]{:S(2)}, u32[]{:S(2)}) collective-permute-start(f32[64,32]{0,1:T(8,128)S(1)} %maximum_select_fusion.15), channel_id=1, source_target_pairs={{0,2},{2,0},{1,3},{3,1},{4,6},{6,4},{5,7},{7,5},{8,10},{10,8},{9,1... | collective-permute-start | bytes 24584 | tf_op jit(solution)/shard_map/ppermute | solution.py:16
  64.9 3.9 %collective-permute-start.9 = (f32[64,64]{0,1:T(8,128)S(1)}, f32[64,64]{0,1:T(8,128)S(1)}, u32[]{:S(2)}, u32[]{:S(2)}) collective-permute-start(f32[64,64]{0,1:T(8,128)S(1)} %maximum_select_fusion.11), channel_id=1, source_target_pairs={{0,4},{4,0},{1,5},{5,1},{2,6},{6,2},{3,7},{7,3},{8,12},{12,8},{9,1... | collective-permute-start | bytes 49160 | tf_op jit(solution)/shard_map/ppermute | solution.py:16
  69.4 4.3 %collective-permute-start.10 = (f32[64,128]{0,1:T(8,128)S(1)}, f32[64,128]{0,1:T(8,128)S(1)}, u32[]{:S(2)}, u32[]{:S(2)}) collective-permute-start(f32[64,128]{0,1:T(8,128)S(1)} %slice_select_fusion.2), channel_id=1, source_target_pairs={{0,8},{8,0},{1,9},{9,1},{2,10},{10,2},{3,11},{11,3},{4,12},{12,4},... | collective-permute-start | bytes 98312 | tf_op jit(solution)/shard_map/ppermute | solution.py:16
  73.8 4.0 %collective-permute-start.11 = (f32[64,64]{0,1:T(8,128)S(1)}, f32[64,64]{0,1:T(8,128)S(1)}, u32[]{:S(2)}, u32[]{:S(2)}) collective-permute-start(f32[64,64]{0,1:T(8,128)S(1)} %slice_select_fusion.4), channel_id=1, source_target_pairs={{0,4},{4,0},{1,5},{5,1},{2,6},{6,2},{3,7},{7,3},{8,12},{12,8},{9,1... | collective-permute-start | bytes 49160 | tf_op jit(solution)/shard_map/ppermute | solution.py:16
  77.7 3.8 %collective-permute-start.12 = (f32[64,32]{0,1:T(8,128)S(1)}, f32[64,32]{0,1:T(8,128)S(1)}, u32[]{:S(2)}, u32[]{:S(2)}) collective-permute-start(f32[64,32]{0,1:T(8,128)S(1)} %slice_select_fusion.7), channel_id=1, source_target_pairs={{0,2},{2,0},{1,3},{3,1},{4,6},{6,4},{5,7},{7,5},{8,10},{10,8},{9,1... | collective-permute-start | bytes 24584 | tf_op jit(solution)/shard_map/ppermute | solution.py:16
  81.6 1.2 collective-permute-start.13
  82.8 1.2 collective-permute-start.14
  84.0 3.7 %collective-permute-start.15 = (f32[64,32]{0,1:T(8,128)S(1)}, f32[64,32]{0,1:T(8,128)S(1)}, u32[]{:S(2)}, u32[]{:S(2)}) collective-permute-start(f32[64,32]{0,1:T(8,128)S(1)} %maximum_select_fusion.16), channel_id=1, source_target_pairs={{0,2},{2,0},{1,3},{3,1},{4,6},{6,4},{5,7},{7,5},{8,10},{10,8},{9,1... | collective-permute-start | bytes 24584 | tf_op jit(solution)/shard_map/ppermute | solution.py:16
  87.7 3.9 %collective-permute-start.16 = (f32[64,64]{0,1:T(8,128)S(1)}, f32[64,64]{0,1:T(8,128)S(1)}, u32[]{:S(2)}, u32[]{:S(2)}) collective-permute-start(f32[64,64]{0,1:T(8,128)S(1)} %maximum_select_fusion.12), channel_id=1, source_target_pairs={{0,4},{4,0},{1,5},{5,1},{2,6},{6,2},{3,7},{7,3},{8,12},{12,8},{9,1... | collective-permute-start | bytes 49160 | tf_op jit(solution)/shard_map/ppermute | solution.py:16
  91.7 4.3 %collective-permute-start.17 = (f32[64,128]{0,1:T(8,128)S(1)}, f32[64,128]{0,1:T(8,128)S(1)}, u32[]{:S(2)}, u32[]{:S(2)}) collective-permute-start(f32[64,128]{0,1:T(8,128)S(1)} %maximum_select_fusion.7), channel_id=1, source_target_pairs={{0,8},{8,0},{1,9},{9,1},{2,10},{10,2},{3,11},{11,3},{4,12},{12,4},... | collective-permute-start | bytes 98312 | tf_op jit(solution)/shard_map/ppermute | solution.py:16
  96.8 7.4 %collective-permute-start.18 = (f32[64,256]{0,1:T(8,128)S(1)}, f32[64,256]{0,1:T(8,128)S(1)}, u32[]{:S(2)}, u32[]{:S(2)}) collective-permute-start(f32[64,256]{0,1:T(8,128)S(1)} %slice_select_fusion), channel_id=1, source_target_pairs={{0,16},{16,0},{1,17},{17,1},{2,18},{18,2},{3,19},{19,3},{4,20},{20... | collective-permute-start | bytes 196616 | tf_op jit(solution)/shard_map/ppermute | solution.py:16
  104.3 4.3 %collective-permute-start.19 = (f32[64,128]{0,1:T(8,128)S(1)}, f32[64,128]{0,1:T(8,128)S(1)}, u32[]{:S(2)}, u32[]{:S(2)}) collective-permute-start(f32[64,128]{0,1:T(8,128)S(1)} %slice_select_fusion.1), channel_id=1, source_target_pairs={{0,8},{8,0},{1,9},{9,1},{2,10},{10,2},{3,11},{11,3},{4,12},{12,4},... | collective-permute-start | bytes 98312 | tf_op jit(solution)/shard_map/ppermute | solution.py:16
  108.6 4.0 %collective-permute-start.20 = (f32[64,64]{0,1:T(8,128)S(1)}, f32[64,64]{0,1:T(8,128)S(1)}, u32[]{:S(2)}, u32[]{:S(2)}) collective-permute-start(f32[64,64]{0,1:T(8,128)S(1)} %slice_select_fusion.3), channel_id=1, source_target_pairs={{0,4},{4,0},{1,5},{5,1},{2,6},{6,2},{3,7},{7,3},{8,12},{12,8},{9,1... | collective-permute-start | bytes 49160 | tf_op jit(solution)/shard_map/ppermute | solution.py:16
  112.6 3.8 %collective-permute-start.21 = (f32[64,32]{0,1:T(8,128)S(1)}, f32[64,32]{0,1:T(8,128)S(1)}, u32[]{:S(2)}, u32[]{:S(2)}) collective-permute-start(f32[64,32]{0,1:T(8,128)S(1)} %slice_select_fusion.6), channel_id=1, source_target_pairs={{0,2},{2,0},{1,3},{3,1},{4,6},{6,4},{5,7},{7,5},{8,10},{10,8},{9,1... | collective-permute-start | bytes 24584 | tf_op jit(solution)/shard_map/ppermute | solution.py:16
  116.4 1.2 collective-permute-start.22
  117.7 1.2 collective-permute-start.23
  118.9 3.7 %collective-permute-start.24 = (f32[64,32]{0,1:T(8,128)S(1)}, f32[64,32]{0,1:T(8,128)S(1)}, u32[]{:S(2)}, u32[]{:S(2)}) collective-permute-start(f32[64,32]{0,1:T(8,128)S(1)} %maximum_select_fusion.17), channel_id=1, source_target_pairs={{0,2},{2,0},{1,3},{3,1},{4,6},{6,4},{5,7},{7,5},{8,10},{10,8},{9,1... | collective-permute-start | bytes 24584 | tf_op jit(solution)/shard_map/ppermute | solution.py:16
  122.6 3.9 %collective-permute-start.25 = (f32[64,64]{0,1:T(8,128)S(1)}, f32[64,64]{0,1:T(8,128)S(1)}, u32[]{:S(2)}, u32[]{:S(2)}) collective-permute-start(f32[64,64]{0,1:T(8,128)S(1)} %maximum_select_fusion.13), channel_id=1, source_target_pairs={{0,4},{4,0},{1,5},{5,1},{2,6},{6,2},{3,7},{7,3},{8,12},{12,8},{9,1... | collective-permute-start | bytes 49160 | tf_op jit(solution)/shard_map/ppermute | solution.py:16
  126.5 4.3 %collective-permute-start.26 = (f32[64,128]{0,1:T(8,128)S(1)}, f32[64,128]{0,1:T(8,128)S(1)}, u32[]{:S(2)}, u32[]{:S(2)}) collective-permute-start(f32[64,128]{0,1:T(8,128)S(1)} %maximum_select_fusion.8), channel_id=1, source_target_pairs={{0,8},{8,0},{1,9},{9,1},{2,10},{10,2},{3,11},{11,3},{4,12},{12,4},... | collective-permute-start | bytes 98312 | tf_op jit(solution)/shard_map/ppermute | solution.py:16
  130.9 7.1 %collective-permute-start.27 = (f32[64,256]{0,1:T(8,128)S(1)}, f32[64,256]{0,1:T(8,128)S(1)}, u32[]{:S(2)}, u32[]{:S(2)}) collective-permute-start(f32[64,256]{0,1:T(8,128)S(1)} %maximum_select_fusion.4), channel_id=1, source_target_pairs={{0,16},{16,0},{1,17},{17,1},{2,18},{18,2},{3,19},{19,3},{4,20},{20... | collective-permute-start | bytes 196616 | tf_op jit(solution)/shard_map/ppermute | solution.py:16
  138.6 1.4 collective-permute-start.28
  140.0 5.6 %collective-permute-start.29 = (f32[64,512]{1,0:T(8,128)S(1)}, f32[64,512]{1,0:T(8,128)S(1)}, u32[]{:S(2)}, u32[]{:S(2)}) collective-permute-start(f32[64,512]{1,0:T(8,128)S(1)} %add.149), channel_id=1, source_target_pairs={{0,2},{2,0},{1,3},{3,1},{4,6},{6,4},{5,7},{7,5},{8,10},{10,8},{9,1... | collective-permute-start | bytes 393224 | tf_op jit(solution)/shard_map/ppermute | solution.py:16
  145.7 5.0 %collective-permute-start.30 = (f32[64,512]{1,0:T(8,128)S(1)}, f32[64,512]{1,0:T(8,128)S(1)}, u32[]{:S(2)}, u32[]{:S(2)}) collective-permute-start(f32[64,512]{1,0:T(8,128)S(1)} %add.150), channel_id=1, source_target_pairs={{0,4},{4,0},{1,5},{5,1},{2,6},{6,2},{3,7},{7,3},{8,12},{12,8},{9,1... | collective-permute-start | bytes 393224 | tf_op jit(solution)/shard_map/ppermute | solution.py:16
  150.7 5.0 %collective-permute-start.31 = (f32[64,512]{1,0:T(8,128)S(1)}, f32[64,512]{1,0:T(8,128)S(1)}, u32[]{:S(2)}, u32[]{:S(2)}) collective-permute-start(f32[64,512]{1,0:T(8,128)S(1)} %add.151), channel_id=1, source_target_pairs={{0,8},{8,0},{1,9},{9,1},{2,10},{10,2},{3,11},{11,3},{4,12},{12,4},... | collective-permute-start | bytes 393224 | tf_op jit(solution)/shard_map/ppermute | solution.py:16
  155.8 6.8 %collective-permute-start.32 = (f32[64,512]{1,0:T(8,128)S(1)}, f32[64,512]{1,0:T(8,128)S(1)}, u32[]{:S(2)}, u32[]{:S(2)}) collective-permute-start(f32[64,512]{1,0:T(8,128)S(1)} %add.152), channel_id=1, source_target_pairs={{0,16},{16,0},{1,17},{17,1},{2,18},{18,2},{3,19},{19,3},{4,20},{20... | collective-permute-start | bytes 393224 | tf_op jit(solution)/shard_map/ppermute | solution.py:16
  163.1 1.3 collective-permute-start.33
  164.4 4.3 %collective-permute-start.34 = (f32[64,256]{1,0:T(8,128)S(1)}, f32[64,256]{1,0:T(8,128)S(1)}, u32[]{:S(2)}, u32[]{:S(2)}) collective-permute-start(f32[64,256]{1,0:T(8,128)S(1)} %add.154), channel_id=1, source_target_pairs={{0,2},{2,0},{1,3},{3,1},{4,6},{6,4},{5,7},{7,5},{8,10},{10,8},{9,1... | collective-permute-start | bytes 196616 | tf_op jit(solution)/shard_map/ppermute | solution.py:16
  168.8 4.3 %collective-permute-start.35 = (f32[64,256]{1,0:T(8,128)S(1)}, f32[64,256]{1,0:T(8,128)S(1)}, u32[]{:S(2)}, u32[]{:S(2)}) collective-permute-start(f32[64,256]{1,0:T(8,128)S(1)} %add.155), channel_id=1, source_target_pairs={{0,4},{4,0},{1,5},{5,1},{2,6},{6,2},{3,7},{7,3},{8,12},{12,8},{9,1... | collective-permute-start | bytes 196616 | tf_op jit(solution)/shard_map/ppermute | solution.py:16
  173.1 4.3 %collective-permute-start.36 = (f32[64,256]{1,0:T(8,128)S(1)}, f32[64,256]{1,0:T(8,128)S(1)}, u32[]{:S(2)}, u32[]{:S(2)}) collective-permute-start(f32[64,256]{1,0:T(8,128)S(1)} %add.156), channel_id=1, source_target_pairs={{0,8},{8,0},{1,9},{9,1},{2,10},{10,2},{3,11},{11,3},{4,12},{12,4},... | collective-permute-start | bytes 196616 | tf_op jit(solution)/shard_map/ppermute | solution.py:16
  177.9 1.3 collective-permute-start.37
  179.2 3.9 %collective-permute-start.38 = (f32[64,128]{1,0:T(8,128)S(1)}, f32[64,128]{1,0:T(8,128)S(1)}, u32[]{:S(2)}, u32[]{:S(2)}) collective-permute-start(f32[64,128]{1,0:T(8,128)S(1)} %add.158), channel_id=1, source_target_pairs={{0,2},{2,0},{1,3},{3,1},{4,6},{6,4},{5,7},{7,5},{8,10},{10,8},{9,1... | collective-permute-start | bytes 98312 | tf_op jit(solution)/shard_map/ppermute | solution.py:16
  183.1 3.9 %collective-permute-start.39 = (f32[64,128]{1,0:T(8,128)S(1)}, f32[64,128]{1,0:T(8,128)S(1)}, u32[]{:S(2)}, u32[]{:S(2)}) collective-permute-start(f32[64,128]{1,0:T(8,128)S(1)} %add.159), channel_id=1, source_target_pairs={{0,4},{4,0},{1,5},{5,1},{2,6},{6,2},{3,7},{7,3},{8,12},{12,8},{9,1... | collective-permute-start | bytes 98312 | tf_op jit(solution)/shard_map/ppermute | solution.py:16
  187.4 1.3 collective-permute-start.40
  188.7 3.9 %collective-permute-start.41 = (f32[64,64]{0,1:T(8,128)S(1)}, f32[64,64]{0,1:T(8,128)S(1)}, u32[]{:S(2)}, u32[]{:S(2)}) collective-permute-start(f32[64,64]{0,1:T(8,128)S(1)} %add.161), channel_id=1, source_target_pairs={{0,2},{2,0},{1,3},{3,1},{4,6},{6,4},{5,7},{7,5},{8,10},{10,8},{9,1... | collective-permute-start | bytes 49160 | tf_op jit(solution)/shard_map/ppermute | solution.py:16
where the time goes:
time: 200 us; the launch traced here: 199 us
  waiting for transfers between devices  143 us (72%)
  starting transfers between devices  25 us (12%)
  matrix products  17.2 us (9%)
  local copies, waits for them, and re-layouts  7.1 us (4%)
  other arithmetic  5.52 us (3%)
    ppermute x42, waiting for transfers between devices, partner(): return lax.ppermute(block, axis, route)  132 us
    ppermute x42, starting transfers between devices, partner(): return lax.ppermute(block, axis, route)  14.9 us
    dot_general x9, matrix products, row_dot(): lax.dot_general(left, right, (((1,), (1,)), ((), ())), precision=HIGH)  8.69 us
    dot_general x10, matrix products, mat_dot(): return jnp.dot(left, right, precision=HIGH)  8.56 us
    all_to_all x1, starting transfers between devices, shards(): lax.all_to_all(send_rows, ('cube', 'front'), split_axis=1, concat_axis=1,...  7.33 us
    all_to_all x1, waiting for transfers between devices, shards(): lax.all_to_all(send_vals, ('cube', 'front'), split_axis=1, concat_axis=1,...  6.73 us
    all_to_all x1, waiting for transfers between devices, shards(): lax.all_to_all(send_rows, ('cube', 'front'), split_axis=1, concat_axis=1,...  4.08 us
  transfers between devices with their start and end apart: 44, of which 44 were waited for; matrix products, arithmetic and copies ran while one was open for 2% of the time, Pallas kernels for 0%

commit v1 on v0

v1 whole, which is shorter than its diff:
```python
import functools
import jax
import jax.numpy as jnp
from jax import lax
from jax.experimental import pallas as pl
from jax.experimental.pallas import tpu as pltpu
from jax.sharding import PartitionSpec as P

F32 = jnp.float32
BF16 = jnp.bfloat16
AXES = ("cube", "front")
MESH = pl.DeviceIdType.MESH

NN = ((1,), (0,))
NT = ((1,), (1,))
TN = ((0,), (0,))


def raw(a, b, dims):
    return lax.dot_general(a, b, (dims, ((), ())), preferred_element_type=F32)


def split(x):
    high = x.astype(BF16)
    return high, (x - high.astype(F32)).astype(BF16)


def mm_split(a, high, low, dims):
    a_high, a_low = split(a)
    rows = a.shape[0]
    both = raw(jnp.concatenate([a_high, a_low], 0), high, dims)
    return both[:rows] + both[rows:] + raw(a_high, low, dims)


def mm(a, b, dims):
    high, low = split(b)
    return mm_split(a, high, low, dims)


def iota(shape, dim):
    return lax.broadcasted_iota(jnp.int32, shape, dim)


def kernel(
    devices, front, sr, sizes, cap, half,
    vals, owner, rows, w1, w2, w3, inv0, inv0_blocks, leaf_inv, leaf_coup,
    leaf_out, sep_out,
    linv, lhigh, llow, sendv, sendi, recvv, recvi, g1, g2, g3, blocks, inv0_other,
    x3, x2, x1, x0, x2s, x1s, x0s, hs, hg, y0,
    lsem, vs, vr, is_, ir, g1s, g1r, g2s, g2r, g3s, g3r, bs, br, hss, hsr, ys, yr, x3ss, x3r, ps, pr,
):
    n0, n1, n2, n3 = sizes
    me = lax.axis_index("cube") * front + lax.axis_index("front")
    m1, m2, m3 = devices // 2, devices // 4, devices // 8
    nrhs = vals.shape[0]
    leaf = leaf_coup.shape[1]
    elems = vals.shape[1]

    def dev(p):
        return (p // front, p % front)

    def partner(bit):
        return me + bit * (1 - 2 * ((me // bit) % 2))

    def remote(src, dst, ssem, rsem, p):
        return pltpu.make_async_remote_copy(
            src_ref=src, dst_ref=dst, send_sem=ssem, recv_sem=rsem,
            device_id=dev(p), device_id_type=MESH)

    fetch = pltpu.make_async_copy(leaf_inv, linv, lsem.at[0])
    fetch.start()

    barrier = pltpu.get_barrier_semaphore()

    def greet(j, _):
        pl.semaphore_signal(barrier, inc=1, device_id=dev((me + j) % devices), device_id_type=MESH)
        return 0

    lax.fori_loop(1, devices, greet, 0)

    own = owner[...]
    marks = iota((devices, elems), 0) == own
    marks_f = jnp.where(marks, 1.0, 0.0).astype(F32)
    earlier = jnp.where(iota((elems, elems), 0) < iota((elems, elems), 1), 1.0, 0.0).astype(BF16)
    before = raw(marks_f.astype(BF16), earlier, NN)
    rank = jnp.sum(before * marks_f, axis=0, keepdims=True).astype(jnp.int32)
    v = vals[...]
    v_a = v.astype(BF16)
    rest = v - v_a.astype(F32)
    v_b = rest.astype(BF16)
    v_c = (rest - v_b.astype(F32)).astype(BF16)
    place = iota((devices * half, elems), 0)
    sides = []
    for side in range(2):
        low = side * half
        target = jnp.where((rank >= low) & (rank < low + half), own * half + rank - low, -1)
        hot = jnp.where(place == target, 1.0, 0.0).astype(BF16)
        sides.append(raw(hot, v_a, NT) + raw(hot, v_b, NT) + raw(hot, v_c, NT))
    sendv[...] = jnp.concatenate(sides, 1).reshape(sendv.shape)
    number = rows[...].astype(F32)
    upper = jnp.floor(number * 0.0078125)
    lower = number - upper * 128.0
    ranks = jnp.where(iota((128, elems), 0) == rank, 1.0, 0.0).astype(BF16)
    sendi[...] = (
        raw((marks_f * upper).astype(BF16), ranks, NT) * 128.0
        + raw((marks_f * lower).astype(BF16), ranks, NT)
    ).reshape(sendi.shape)
    recvv[me] = sendv[me]
    recvi[me] = sendi[me]

    pl.semaphore_wait(barrier, devices - 1)

    def load_copies(p, slot, sem):
        return (
            remote(sendv.at[p], recvv.at[slot], vs.at[p], vr.at[sem], p),
            remote(sendi.at[p], recvi.at[slot], is_.at[p], ir.at[sem], p),
        )

    def send_loads(j, _):
        for copy in load_copies((me + j) % devices, me, me):
            copy.start()
        return 0

    lax.fori_loop(1, devices, send_loads, 0)

    def group_copy(src, dst, ssem, rsem, size, j, arriving):
        p = me // size * size + (me + j) % size
        slot = p % size if arriving else me % size
        return remote(src, dst.at[slot], ssem.at[p % size], rsem.at[slot], p)

    def group(src, dst, ssem, rsem, size, act):
        def body(j, _):
            copy = group_copy(src, dst, ssem, rsem, size, j, act != "start")
            if act == "start":
                copy.start()
            elif act == "recv":
                copy.wait_recv()
            else:
                copy.wait_send()
            return 0
        lax.fori_loop(1, size, body, 0)

    other0 = partner(m1)
    inv0_copy = remote(inv0, inv0_other, ps.at[0], pr.at[0], other0)

    group(w3, g3, g3s, g3r, m3, "start")
    group(w2, g2, g2s, g2r, m2, "start")
    inv0_copy.start()
    group(w1, g1, g1s, g1r, m1, "start")

    def block_copy(j, arriving):
        p = (me + j) % devices
        slot = p if arriving else me
        return remote(inv0_blocks.at[p], blocks.at[slot], bs.at[p], br.at[slot], p)

    def send_block(j, _):
        block_copy(j, False).start()
        return 0

    lax.fori_loop(1, devices, send_block, 0)
    g1[me % m1] = w1[...]
    g2[me % m2] = w2[...]
    g3[me % m3] = w3[...]
    blocks[me] = inv0_blocks[me]

    fetch.wait()
    linv_value = linv[...]
    high = linv_value.astype(BF16)
    lhigh[...] = high
    llow[...] = (linv_value - high.astype(F32)).astype(BF16)

    def get_loads(j, _):
        p = (me + j) % devices
        for copy in load_copies(p, p, p):
            copy.wait_recv()
        return 0

    lax.fori_loop(1, devices, get_loads, 0)

    slots = devices * half
    arrived = jnp.transpose(recvv[...].reshape(slots, 128))
    pick = jnp.where(iota((slots, devices), 0) // half == iota((slots, devices), 1), 1.0, 0.0).astype(BF16)
    ids = recvi[...].reshape(devices, 128)
    ids_up = jnp.floor(ids * 0.0078125)
    ids_low = ids - ids_up * 128.0
    spread = raw(pick, ids_up.astype(BF16), NN) * 128.0 + raw(pick, ids_low.astype(BF16), NN)
    lane = iota((slots, 128), 1)
    turn = iota((slots, 128), 0) % half
    loads = None
    for side in range(2):
        row = jnp.sum(jnp.where(lane == turn + side * half, spread, 0.0), axis=1, keepdims=True)
        hot = jnp.where(iota((slots, leaf), 1) == row.astype(jnp.int32), 1.0, 0.0).astype(BF16)
        part_high, part_low = split(arrived[side * nrhs:(side + 1) * nrhs])
        both = raw(jnp.concatenate([part_high, part_low], 0), hot, NN)
        term = both[:nrhs] + both[nrhs:]
        loads = term if loads is None else loads + term
    leaf_y = mm_split(loads, lhigh[...], llow[...], NT)
    coup = leaf_coup[...]
    x3[me % m3] = mm(leaf_y, coup, NT)
    group(x3.at[me % m3], x3, x3ss, x3r, m3, "start")

    group(w3, g3, g3s, g3r, m3, "recv")
    group(w2, g2, g2s, g2r, m2, "recv")
    c2t = g3[:, :, :n2].reshape(m3 * sr, n2)
    inv3 = g3[:, :, n2:n2 + n3].reshape(m3 * sr, n3)
    s3 = jnp.transpose(g3[:, :, n2 + n3:].reshape(m3 * sr, nrhs))
    c1t = g2[:, :, :n1].reshape(m2 * sr, n1)
    inv2 = g2[:, :, n1:n1 + n2].reshape(m2 * sr, n2)
    s2 = jnp.transpose(g2[:, :, n1 + n2:n1 + n2 + nrhs].reshape(m2 * sr, nrhs))


    def get_x3(j, _):
        p = me // m3 * m3 + (me + j) % m3
        remote(x3.at[me % m3], x3.at[p % m3], x3ss.at[p % m3], x3r.at[p % m3], p).wait_recv()
        return 0

    lax.fori_loop(1, m3, get_x3, 0)
    y3 = mm(s3 - jnp.sum(x3[...], axis=0), inv3, NT)
    t2 = mm(y3, c2t, NN)
    x2s[...] = t2
    copy2 = remote(x2s, x2, ps.at[1], pr.at[1], partner(m3))
    copy2.start()

    group(w1, g1, g1s, g1r, m1, "recv")
    inv0_copy.wait_recv()
    c0t = g1[:, :, :n0].reshape(m1 * sr, n0)
    pair0 = jnp.concatenate([inv0[...], inv0_other[...]], 0)
    hmat = mm(pair0, c0t, NT)
    hs[...] = hmat
    hg[me % m1] = hmat
    group(hs, hg, hss, hsr, m1, "start")

    copy2.wait_recv()
    y2 = mm(s2 - t2 - x2[...], inv2, NT)
    t1 = mm(y2, c1t, NN)
    x1s[...] = t1
    copy1 = remote(x1s, x1, ps.at[2], pr.at[2], partner(m2))
    copy1.start()

    inv1 = g1[:, :, n0:n0 + n1].reshape(m1 * sr, n1)
    s01 = g1[:, :, n0 + n1:].reshape(m1 * sr, 2 * nrhs)
    s1 = jnp.transpose(s01[:, nrhs:])
    second = me // m1 == 1
    mine0 = jnp.where(second, pair0[:, n1:], pair0[:, :n1])
    base = mm(mine0, s01[:, :nrhs], NN)

    copy1.wait_recv()
    y1 = mm(s1 - t1 - x1[...], inv1, NT)
    part = base - mm(hmat, y1, NT)
    eight = sr // 2
    x0s[...] = jnp.concatenate([part[sr:sr + eight], part[sr + eight:]], 1)
    copy0 = remote(x0s, x0, ps.at[3], pr.at[3], other0)
    copy0.start()
    copy0.wait_recv()
    y0[me] = jnp.concatenate([part[:eight], part[eight:sr]], 1) + x0[...]

    def y_copy(j, arriving):
        p = (me + j) % devices
        slot = p if arriving else me
        return remote(y0.at[me], y0.at[slot], ys.at[p], yr.at[slot], p)

    def send_y(j, _):
        y_copy(j, False).start()
        return 0

    lax.fori_loop(1, devices, send_y, 0)
    group(hs, hg, hss, hsr, m1, "recv")

    def get_block(j, _):
        block_copy(j, True).wait_recv()
        return 0

    lax.fori_loop(1, devices, get_block, 0)

    def get_y(j, _):
        y_copy(j, True).wait_recv()
        return 0

    lax.fori_loop(1, devices, get_y, 0)

    z1 = y1
    for far in range(2):
        where_ = (me // m1 + far) % 2 * m1
        turned = jnp.transpose(y0[pl.ds(where_, m1)].reshape(m1 * eight, 2 * nrhs))
        for side in range(2):
            piece = hg[:, far * sr + side * eight:far * sr + (side + 1) * eight, :].reshape(m1 * eight, n1)
            z1 = z1 - mm(turned[side * nrhs:(side + 1) * nrhs], piece, NN)

    sol1 = mm(z1, inv1, NN)
    sol2 = mm(y2 - mm(sol1, c1t, NT), inv2, NN)
    sol3 = mm(y3 - mm(sol2, c2t, NT), inv3, NN)
    leaf_out[...] = mm_split(leaf_y - mm(sol3, coup, NN), lhigh[...], llow[...], NN)

    full = jnp.transpose(y0[...].reshape(devices * eight, 2 * nrhs))
    sol0 = None
    for side in range(2):
        piece = blocks[:, side * eight:(side + 1) * eight, :].reshape(devices * eight, sr)
        term = mm(full[side * nrhs:(side + 1) * nrhs], piece, NN)
        sol0 = term if sol0 is None else sol0 + term
    sep_out[0] = sol0
    for level, value, size in ((1, sol1, m1), (2, sol2, m2), (3, sol3, m3)):
        wide = value.shape[1]
        chosen = jnp.where(iota((wide, sr), 0) == me % size * sr + iota((wide, sr), 1), 1.0, 0.0).astype(BF16)
        a = value.astype(BF16)
        left = value - a.astype(F32)
        b = left.astype(BF16)
        c = (left - b.astype(F32)).astype(BF16)
        sep_out[level] = raw(a, chosen, NN) + raw(b, chosen, NN) + raw(c, chosen, NN)

    def sent(j, _):
        p = (me + j) % devices
        for copy in load_copies(p, me, me):
            copy.wait_send()
        block_copy(j, False).wait_send()
        y_copy(j, False).wait_send()
        return 0

    lax.fori_loop(1, devices, sent, 0)
    group(w3, g3, g3s, g3r, m3, "sent")
    group(w2, g2, g2s, g2r, m2, "sent")
    group(w1, g1, g1s, g1r, m1, "sent")
    group(hs, hg, hss, hsr, m1, "sent")

    def sent_x3(j, _):
        p = me // m3 * m3 + (me + j) % m3
        remote(x3.at[me % m3], x3.at[me % m3], x3ss.at[p % m3], x3r.at[me % m3], p).wait_send()
        return 0

    lax.fori_loop(1, m3, sent_x3, 0)
    for copy in (inv0_copy, copy2, copy1, copy0):
        copy.wait_send()


def shards(
    elem_loads, elem_owner, elem_row, sep_loads, leaf_inverse, leaf_coupling,
    coupling0, coupling1, coupling2, inverse0, inverse1, inverse2, inverse3,
):
    front = lax.axis_size("front")
    devices = lax.axis_size(AXES)
    nrhs, elems = elem_loads.shape
    leaf = leaf_inverse.shape[0]
    sr = sep_loads.shape[2]
    sizes = (inverse0.shape[1], inverse1.shape[1], inverse2.shape[1], inverse3.shape[1])
    n0, n1, n2, n3 = sizes
    cap = 2 * elems // devices
    half = max(8, -(-cap // 16) * 8)
    m1, m2, m3 = devices // 2, devices // 4, devices // 8
    turned = jnp.transpose(sep_loads, (2, 0, 1))
    w1 = jnp.concatenate([coupling0.T, inverse1, turned[:, 0], turned[:, 1]], 1)
    w2 = jnp.concatenate([coupling1.T, inverse2, turned[:, 2], turned[:, 2]], 1)
    w3 = jnp.concatenate([coupling2.T, inverse3, turned[:, 3]], 1)
    blocks = jnp.transpose(inverse0.reshape(sr, devices, sr), (1, 0, 2))
    vmem = pl.BlockSpec(memory_space=pltpu.VMEM)
    dma = pltpu.SemaphoreType.DMA
    V = pltpu.VMEM
    return tuple(pl.pallas_call(
        functools.partial(kernel, devices, front, sr, sizes, cap, half),
        out_shape=(
            jax.ShapeDtypeStruct((nrhs, leaf), F32),
            jax.ShapeDtypeStruct(sep_loads.shape, F32),
        ),
        in_specs=[vmem] * 8 + [pl.BlockSpec(memory_space=pl.ANY), vmem],
        out_specs=(vmem, vmem),
        scratch_shapes=[
            V((leaf, leaf), F32), V((leaf, leaf), BF16), V((leaf, leaf), BF16),
            V((devices, half, 2 * nrhs), F32), V((devices, 1, 128), F32),
            V((devices, half, 2 * nrhs), F32), V((devices, 1, 128), F32),
            V((m1, *w1.shape), F32), V((m2, *w2.shape), F32), V((m3, *w3.shape), F32),
            V((devices, sr, sr), F32), V((sr, n0), F32),
            V((m3, nrhs, n3), F32), V((nrhs, n2), F32), V((nrhs, n1), F32), V((sr // 2, 2 * nrhs), F32),
            V((nrhs, n2), F32), V((nrhs, n1), F32), V((sr // 2, 2 * nrhs), F32),
            V((2 * sr, n1), F32), V((m1, 2 * sr, n1), F32), V((devices, sr // 2, 2 * nrhs), F32),
            dma((1,)), dma((devices,)), dma((devices,)), dma((devices,)), dma((devices,)),
            dma((m1,)), dma((m1,)), dma((m2,)), dma((m2,)), dma((m3,)), dma((m3,)),
            dma((devices,)), dma((devices,)), dma((m1,)), dma((m1,)), dma((devices,)), dma((devices,)),
            dma((m3,)), dma((m3,)), dma((4,)), dma((4,)),
        ],
        compiler_params=pltpu.CompilerParams(
            collective_id=0, has_side_effects=True, vmem_limit_bytes=60 * 1024 * 1024),
    )(elem_loads, elem_owner.reshape(1, elems), elem_row.reshape(1, elems), w1, w2, w3,
      inverse0, blocks, leaf_inverse, leaf_coupling))


def solution(mesh):
    in_specs = (
        P(None, AXES), P(AXES, None), P(AXES), P(None, None, AXES), P(AXES, None), P(None, AXES),
        P(None, AXES), P(None, AXES), P(None, AXES),
        P(AXES, None), P(AXES, None), P(AXES, None), P(AXES, None),
    )
    out_specs = (P(None, AXES), P(None, None, AXES))
    return jax.shard_map(shards, mesh=mesh, in_specs=in_specs, out_specs=out_specs, check_vma=False)
```

time: 200 us -> 67.4 us (0.34)
  waiting for transfers between devices: 143 us -> 0 us
  Pallas kernels: 0 us -> 56.1 us
  starting transfers between devices: 25 us -> 0 us
  matrix products: 17.2 us -> 0 us
    ppermute x42 -> x0, waiting for transfers between devices: 132 us -> none  [partner(): return lax.ppermute(block, axis, route)]
    pallas_call x0 -> x1, Pallas kernels: none -> 56.1 us  [shards(): pl.pallas_call(functools.partial(kernel, devices, front, sr, sizes, cap,...]
    dot_general x19 -> x0, matrix products: 17.2 us -> none  [the longest x9 8.69 us: row_dot(): lax.dot_general(left, right, (((1,), (1,)), ((), ())), precision=HIGH)]
    ppermute x42 -> x0, starting transfers between devices: 14.9 us -> none  [partner(): return lax.ppermute(block, axis, route)]
    all_to_all x2 -> x0, waiting for transfers between devices: 10.8 us -> none  [the longest x1 6.73 us: shards(): lax.all_to_all(send_vals, ('cube', 'front'), split_axis=1, concat_axis=1,...]
    all_to_all x2 -> x0, starting transfers between devices: 10.1 us -> none  [the longest x1 7.33 us: shards(): lax.all_to_all(send_rows, ('cube', 'front'), split_axis=1, concat_axis=1,...]
    concatenate x0 -> x3, other arithmetic: none -> 4.27 us  [the longest x1 1.47 us: shards(): w1 = jnp.concatenate([coupling0.T, inverse1, turned[:, 0], turned[:, 1]], 1)]
    scatter x2 -> x0, local copies, waits for them, and re-layouts: 2.77 us -> none  [the longest x1 1.55 us: shards(): jnp.full((1, devices * capacity), -1, jnp.int32).at[0, slots].set(elem_row)]
  transfers between devices with their start and end apart: 44 -> 0, of which waited for: 44 -> 0; matrix products, arithmetic and copies ran while one was open for 2% -> 0% of each run, Pallas kernels for 0% -> 0%
where the time goes in v1:
time: 67.4 us; the launch traced here: 66.8 us
  Pallas kernels  56.1 us (83%)
  local copies, waits for them, and re-layouts  5.76 us (9%)
  other arithmetic  4.27 us (6%)
    pallas_call x1, Pallas kernels, shards(): pl.pallas_call(functools.partial(kernel, devices, front, sr, sizes, cap,...  56.1 us
    reshape x2, local copies, waits for them, and re-layouts, shards(): blocks = jnp.transpose(inverse0.reshape(sr, devices, sr), (1, 0, 2))  1.74 us
    unnamed x1, local copies, waits for them, and re-layouts  1.67 us
    pallas_call x1, local copies, waits for them, and re-layouts, shards(): pl.pallas_call(functools.partial(kernel, devices, front, sr, sizes, cap,...  1.61 us
    concatenate x1, other arithmetic, shards(): w1 = jnp.concatenate([coupling0.T, inverse1, turned[:, 0], turned[:, 1]], 1)  1.47 us
    concatenate x1, other arithmetic, shards(): w2 = jnp.concatenate([coupling1.T, inverse2, turned[:, 2], turned[:, 2]], 1)  1.42 us
    concatenate x1, other arithmetic, shards(): w3 = jnp.concatenate([coupling2.T, inverse3, turned[:, 3]], 1)  1.38 us

profile of v1, /device:TPU:0, one launch (start us, length us, event | category | flops | bytes accessed | tf_op | source)
XLA Modules:
  0.0 66.8 jit_solution(3683803104813324089)
XLA Ops:
  0.6 0.8 %slice_bitcast_fusion = (f32[16,64]{1,0:T(8,128)S(1)}, f32[16,64]{1,0:T(8,128)S(1)}, f32[16,64]{1,0:T(8,128)S(1)}, f32[16,64]{1,0:T(8,128)S(1)}) fusion(f32[16,4,64]{2,0,1:T(8,128)} %bitcast.18), kind=kLoop, calls=%fused_computation.4 | loop fusion | bytes 32768 | tf_op jit(solution)/shard_map/squeeze | solution.py:351
  1.4 1.4 %pad_maximum_fusion.2.w3 = f32[16,256]{1,0:T(8,128)} fusion(f32[16,64]{1,0:T(8,128)S(1)} %get-tuple-element.6, f32[16,64]{1,0:T(8,128)} %param.25, f32[16,128]{1,0:T(8,128)} %bitcast.21), kind=kLoop, calls=%fused_computation.3 | loop fusion | flops 8192 | bytes 32768 | tf_op jit(solution)/shard_map/concatenate | solution.py:351
  2.8 1.4 %pad_maximum_fusion.1.w2 = f32[16,512]{1,0:T(8,128)} fusion(f32[16,64]{1,0:T(8,128)S(1)} %get-tuple-element.7, f32[16,128]{1,0:T(8,128)} %param.24, f32[16,256]{1,0:T(8,128)} %bitcast.20), kind=kLoop, calls=%fused_computation.2 | loop fusion | flops 24576 | bytes 61440 | tf_op jit(solution)/shard_map/concatenate | solution.py:350
  4.2 1.5 %pad_maximum_fusion.w1 = f32[16,896]{1,0:T(8,128)} fusion(f32[16,64]{1,0:T(8,128)S(1)} %get-tuple-element.8, f32[16,64]{1,0:T(8,128)S(1)} %get-tuple-element.9, f32[16,256]{1,0:T(8,128)} %param.23, f32[16,512]{1,0:T(8,128)} %bitcast.19), kind=kLoop, calls=%fused_computation.1 | loop fusion | flops 43008 | bytes 114688 | tf_op jit(solution)/shard_map/concatenate | solution.py:349
  5.7 0.9 %reshape.15 = f32[16,32,16]{2,1,0:T(8,128)S(1)} reshape(f32[16,512]{1,0:T(8,128)} %inv0.1) | data formatting | bytes 65536 | tf_op jit(solution)/shard_map/reshape | solution.py:352
  6.5 0.9 %copy.19 = f32[16,32,16]{2,0,1:T(8,128)} copy(f32[16,32,16]{2,1,0:T(8,128)S(1)} %reshape.15) | data formatting | bytes 65536 | tf_op jit(solution)/shard_map/reshape | solution.py:352
  7.4 56.1 %shard_map.140 = (f32[64,1024]{1,0:T(8,128)}, f32[4,64,16]{2,1,0:T(8,128)}) custom-call(f32[64,256]{1,0:T(8,128)} %vals.1, s32[1,256]{1,0:T(1,128)} %bitcast.22, s32[1,256]{1,0:T(1,128)} %bitcast.23, f32[16,896]{1,0:T(8,128)} %pad_maximum_fusion.w1, f32[16,512]{1,0:T(8,128)} %pad_maximum_fusion.1.w2, f32[16,256]{1,0:T(8,128)} %pad_maximum_fusion.2.w3, ...), custom_call_target="tpu_custom_call" | custom-call | tf_op jit(solution)/shard_map/pallas_call | solution.py:356
  63.5 1.6 %copy.17 = f32[4,64,16]{1,2,0:T(8,128)} copy(f32[4,64,16]{2,1,0:T(8,128)} %get-tuple-element.5) | data formatting | bytes 32768 | tf_op jit(solution)/shard_map/pallas_call | solution.py:356
  65.1 1.7 %copy.21 = f32[64,1024]{1,0:T(8,128)} copy(f32[64,1024]{1,0:T(8,128)} %get-tuple-element.12) | data formatting | bytes 524288

commit v2 on v1

--- a/solution.py
+++ b/solution.py
@@ -43,11 +43,11 @@
 
 def kernel(
     devices, front, sr, sizes, cap, half,
-    vals, owner, rows, w1, w2, w3, inv0, inv0_blocks, leaf_inv, leaf_coup,
+    vals, owner, rows, sep, inv0, inv1_own, inv2_own, inv3_own, coup0, coup1, coup2, leaf_inv, leaf_coup,
     leaf_out, sep_out,
-    linv, lhigh, llow, sendv, sendi, recvv, recvi, g1, g2, g3, blocks, inv0_other,
-    x3, x2, x1, x0, x2s, x1s, x0s, hs, hg, y0,
-    lsem, vs, vr, is_, ir, g1s, g1r, g2s, g2r, g3s, g3r, bs, br, hss, hsr, ys, yr, x3ss, x3r, ps, pr,
+    linv, lhigh, llow, sendv, sendi, recvv, recvi, g1, g2, g3, inv0_blocks, blocks, inv0_other,
+    x3, x2, x1, x0, x2s, x1s, x0s, hg, y0,
+    lsem, vs, vr, is_, ir, g1s, g1r, g2s, g2r, g3s, g3r, bs, br, hss, hsr, ys, yr, x3ss, x3r, ps, pr, g1f, hf,
 ):
     n0, n1, n2, n3 = sizes
     me = lax.axis_index("cube") * front + lax.axis_index("front")
@@ -78,7 +78,8 @@
 
     lax.fori_loop(1, devices, greet, 0)
 
-    own = owner[...]
+    eye = iota((elems, elems), 0) == iota((elems, elems), 1)
+    own = jnp.sum(jnp.where(eye, owner[...], 0), axis=0, keepdims=True)
     marks = iota((devices, elems), 0) == own
     marks_f = jnp.where(marks, 1.0, 0.0).astype(F32)
     earlier = jnp.where(iota((elems, elems), 0) < iota((elems, elems), 1), 1.0, 0.0).astype(BF16)
@@ -105,6 +106,11 @@
         raw((marks_f * upper).astype(BF16), ranks, NT) * 128.0
         + raw((marks_f * lower).astype(BF16), ranks, NT)
     ).reshape(sendi.shape)
+    g1[me % m1] = jnp.concatenate(
+        [jnp.transpose(coup0[...]), inv1_own[...], jnp.transpose(sep[0]), jnp.transpose(sep[1])], 1)
+    own2 = jnp.transpose(sep[2])
+    g2[me % m2] = jnp.concatenate([jnp.transpose(coup1[...]), inv2_own[...], own2, own2], 1)
+    g3[me % m3] = jnp.concatenate([jnp.transpose(coup2[...]), inv3_own[...], jnp.transpose(sep[3])], 1)
     recvv[me] = sendv[me]
     recvi[me] = sendi[me]
 
@@ -143,10 +149,46 @@
     other0 = partner(m1)
     inv0_copy = remote(inv0, inv0_other, ps.at[0], pr.at[0], other0)
 
-    group(w3, g3, g3s, g3r, m3, "start")
-    group(w2, g2, g2s, g2r, m2, "start")
+    group(g3.at[me % m3], g3, g3s, g3r, m3, "start")
+    group(g2.at[me % m2], g2, g2s, g2r, m2, "start")
     inv0_copy.start()
-    group(w1, g1, g1s, g1r, m1, "start")
+    twin = partner(1)
+
+    def wide(dst, ssem, rsem, fsem, act):
+        start = me // m1 * m1
+
+        def slot_of(first, j):
+            return (first % m1 + front * j) % m1
+
+        def direct(j, _):
+            slot = slot_of(me, j)
+            if act == "start":
+                remote(dst.at[me % m1], dst.at[me % m1], ssem.at[slot], rsem.at[me % m1], start + slot).start()
+            elif act == "sent":
+                remote(dst.at[me % m1], dst.at[me % m1], ssem.at[slot], rsem.at[me % m1], start + slot).wait_send()
+            elif act == "pass":
+                remote(dst.at[slot], dst.at[slot], ssem.at[slot], rsem.at[slot], start + slot).wait_recv()
+                remote(dst.at[slot], dst.at[slot], fsem.at[slot], rsem.at[slot], twin).start()
+            return 0
+
+        def passed(j, _):
+            if act == "sent":
+                slot = slot_of(me, j)
+                remote(dst.at[slot], dst.at[slot], fsem.at[slot], rsem.at[slot], twin).wait_send()
+            else:
+                slot = slot_of(twin, j)
+                remote(dst.at[slot], dst.at[slot], fsem.at[slot], rsem.at[slot], twin).wait_recv()
+            return 0
+
+        if act == "start":
+            mine = me % m1
+            remote(dst.at[mine], dst.at[mine], fsem.at[mine], rsem.at[mine], twin).start()
+        if act != "recv":
+            lax.fori_loop(1, m1 // front, direct, 0)
+        if act in ("recv", "sent"):
+            lax.fori_loop(0, m1 // front, passed, 0)
+
+    wide(g1, g1s, g1r, g1f, "start")
 
     def block_copy(j, arriving):
         p = (me + j) % devices
@@ -157,10 +199,9 @@
         block_copy(j, False).start()
         return 0
 
-    lax.fori_loop(1, devices, send_block, 0)
-    g1[me % m1] = w1[...]
-    g2[me % m2] = w2[...]
-    g3[me % m3] = w3[...]
+    inv0_value = inv0[...]
+    for p in range(devices):
+        inv0_blocks[p] = inv0_value[:, p * sr:(p + 1) * sr]
     blocks[me] = inv0_blocks[me]
 
     fetch.wait()
@@ -199,8 +240,8 @@
     x3[me % m3] = mm(leaf_y, coup, NT)
     group(x3.at[me % m3], x3, x3ss, x3r, m3, "start")
 
-    group(w3, g3, g3s, g3r, m3, "recv")
-    group(w2, g2, g2s, g2r, m2, "recv")
+    group(g3.at[me % m3], g3, g3s, g3r, m3, "recv")
+    group(g2.at[me % m2], g2, g2s, g2r, m2, "recv")
     c2t = g3[:, :, :n2].reshape(m3 * sr, n2)
     inv3 = g3[:, :, n2:n2 + n3].reshape(m3 * sr, n3)
     s3 = jnp.transpose(g3[:, :, n2 + n3:].reshape(m3 * sr, nrhs))
@@ -221,14 +262,7 @@
     copy2 = remote(x2s, x2, ps.at[1], pr.at[1], partner(m3))
     copy2.start()
 
-    group(w1, g1, g1s, g1r, m1, "recv")
-    inv0_copy.wait_recv()
-    c0t = g1[:, :, :n0].reshape(m1 * sr, n0)
-    pair0 = jnp.concatenate([inv0[...], inv0_other[...]], 0)
-    hmat = mm(pair0, c0t, NT)
-    hs[...] = hmat
-    hg[me % m1] = hmat
-    group(hs, hg, hss, hsr, m1, "start")
+    wide(g1, g1s, g1r, g1f, "pass")
 
     copy2.wait_recv()
     y2 = mm(s2 - t2 - x2[...], inv2, NT)
@@ -237,6 +271,13 @@
     copy1 = remote(x1s, x1, ps.at[2], pr.at[2], partner(m2))
     copy1.start()
 
+    wide(g1, g1s, g1r, g1f, "recv")
+    inv0_copy.wait_recv()
+    c0t = g1[:, :, :n0].reshape(m1 * sr, n0)
+    pair0 = jnp.concatenate([inv0[...], inv0_other[...]], 0)
+    hmat = mm(pair0, c0t, NT)
+    hg[me % m1] = hmat
+    wide(hg, hss, hsr, hf, "start")
     inv1 = g1[:, :, n0:n0 + n1].reshape(m1 * sr, n1)
     s01 = g1[:, :, n0 + n1:].reshape(m1 * sr, 2 * nrhs)
     s1 = jnp.transpose(s01[:, nrhs:])
@@ -264,19 +305,19 @@
         return 0
 
     lax.fori_loop(1, devices, send_y, 0)
-    group(hs, hg, hss, hsr, m1, "recv")
+    wide(hg, hss, hsr, hf, "pass")
+    lax.fori_loop(1, devices, send_block, 0)
 
     def get_block(j, _):
         block_copy(j, True).wait_recv()
         return 0
 
-    lax.fori_loop(1, devices, get_block, 0)
-
     def get_y(j, _):
         y_copy(j, True).wait_recv()
         return 0
 
     lax.fori_loop(1, devices, get_y, 0)
+    wide(hg, hss, hsr, hf, "recv")
 
     z1 = y1
     for far in range(2):
@@ -291,6 +332,7 @@
     sol3 = mm(y3 - mm(sol2, c2t, NT), inv3, NN)
     leaf_out[...] = mm_split(leaf_y - mm(sol3, coup, NN), lhigh[...], llow[...], NN)
 
+    lax.fori_loop(1, devices, get_block, 0)
     full = jnp.transpose(y0[...].reshape(devices * eight, 2 * nrhs))
     sol0 = None
     for side in range(2):
@@ -299,8 +341,8 @@
         sol0 = term if sol0 is None else sol0 + term
     sep_out[0] = sol0
     for level, value, size in ((1, sol1, m1), (2, sol2, m2), (3, sol3, m3)):
-        wide = value.shape[1]
-        chosen = jnp.where(iota((wide, sr), 0) == me % size * sr + iota((wide, sr), 1), 1.0, 0.0).astype(BF16)
+        width = value.shape[1]
+        chosen = jnp.where(iota((width, sr), 0) == me % size * sr + iota((width, sr), 1), 1.0, 0.0).astype(BF16)
         a = value.astype(BF16)
         left = value - a.astype(F32)
         b = left.astype(BF16)
@@ -316,10 +358,10 @@
         return 0
 
     lax.fori_loop(1, devices, sent, 0)
-    group(w3, g3, g3s, g3r, m3, "sent")
-    group(w2, g2, g2s, g2r, m2, "sent")
-    group(w1, g1, g1s, g1r, m1, "sent")
-    group(hs, hg, hss, hsr, m1, "sent")
+    group(g3.at[me % m3], g3, g3s, g3r, m3, "sent")
+    group(g2.at[me % m2], g2, g2s, g2r, m2, "sent")
+    wide(g1, g1s, g1r, g1f, "sent")
+    wide(hg, hss, hsr, hf, "sent")
 
     def sent_x3(j, _):
         p = me // m3 * m3 + (me + j) % m3
@@ -345,11 +387,7 @@
     cap = 2 * elems // devices
     half = max(8, -(-cap // 16) * 8)
     m1, m2, m3 = devices // 2, devices // 4, devices // 8
-    turned = jnp.transpose(sep_loads, (2, 0, 1))
-    w1 = jnp.concatenate([coupling0.T, inverse1, turned[:, 0], turned[:, 1]], 1)
-    w2 = jnp.concatenate([coupling1.T, inverse2, turned[:, 2], turned[:, 2]], 1)
-    w3 = jnp.concatenate([coupling2.T, inverse3, turned[:, 3]], 1)
-    blocks = jnp.transpose(inverse0.reshape(sr, devices, sr), (1, 0, 2))
+    pad = 2 * nrhs
     vmem = pl.BlockSpec(memory_space=pltpu.VMEM)
     dma = pltpu.SemaphoreType.DMA
     V = pltpu.VMEM
@@ -359,26 +397,28 @@
             jax.ShapeDtypeStruct((nrhs, leaf), F32),
             jax.ShapeDtypeStruct(sep_loads.shape, F32),
         ),
-        in_specs=[vmem] * 8 + [pl.BlockSpec(memory_space=pl.ANY), vmem],
+        in_specs=[vmem] * 11 + [pl.BlockSpec(memory_space=pl.ANY), vmem],
         out_specs=(vmem, vmem),
         scratch_shapes=[
             V((leaf, leaf), F32), V((leaf, leaf), BF16), V((leaf, leaf), BF16),
             V((devices, half, 2 * nrhs), F32), V((devices, 1, 128), F32),
             V((devices, half, 2 * nrhs), F32), V((devices, 1, 128), F32),
-            V((m1, *w1.shape), F32), V((m2, *w2.shape), F32), V((m3, *w3.shape), F32),
+            V((m1, sr, n0 + n1 + pad), F32), V((m2, sr, n1 + n2 + pad), F32), V((m3, sr, n2 + n3 + nrhs), F32),
+            V((devices, sr, sr), F32),
             V((devices, sr, sr), F32), V((sr, n0), F32),
             V((m3, nrhs, n3), F32), V((nrhs, n2), F32), V((nrhs, n1), F32), V((sr // 2, 2 * nrhs), F32),
             V((nrhs, n2), F32), V((nrhs, n1), F32), V((sr // 2, 2 * nrhs), F32),
-            V((2 * sr, n1), F32), V((m1, 2 * sr, n1), F32), V((devices, sr // 2, 2 * nrhs), F32),
+            V((m1, 2 * sr, n1), F32), V((devices, sr // 2, 2 * nrhs), F32),
             dma((1,)), dma((devices,)), dma((devices,)), dma((devices,)), dma((devices,)),
             dma((m1,)), dma((m1,)), dma((m2,)), dma((m2,)), dma((m3,)), dma((m3,)),
             dma((devices,)), dma((devices,)), dma((m1,)), dma((m1,)), dma((devices,)), dma((devices,)),
-            dma((m3,)), dma((m3,)), dma((4,)), dma((4,)),
+            dma((m3,)), dma((m3,)), dma((4,)), dma((4,)), dma((m1,)), dma((m1,)),
         ],
         compiler_params=pltpu.CompilerParams(
             collective_id=0, has_side_effects=True, vmem_limit_bytes=60 * 1024 * 1024),
-    )(elem_loads, elem_owner.reshape(1, elems), elem_row.reshape(1, elems), w1, w2, w3,
-      inverse0, blocks, leaf_inverse, leaf_coupling))
+    )(elem_loads, elem_owner, elem_row.reshape(1, elems), sep_loads,
+      inverse0, inverse1, inverse2, inverse3, coupling0, coupling1, coupling2,
+      leaf_inverse, leaf_coupling))
 
 
 def solution(mesh):

time: 67.4 us -> 57.4 us (0.85)
  Pallas kernels: 56.1 us -> 45.6 us
  local copies, waits for them, and re-layouts: 5.76 us -> 10.7 us
  other arithmetic: 4.27 us -> 0 us
    pallas_call x1, Pallas kernels: 56.1 us -> 45.6 us  [shards(): pl.pallas_call(functools.partial(kernel, devices, front, sr, sizes, cap,...]
    unnamed x1 -> x6, local copies, waits for them, and re-layouts: 1.67 us -> 9.13 us
    concatenate x3 -> x0, other arithmetic: 4.27 us -> none  [the longest x1 1.47 us: shards(): w1 = jnp.concatenate([coupling0.T, inverse1, turned[:, 0], turned[:, 1]], 1)]
    reshape x2 -> x0, local copies, waits for them, and re-layouts: 1.74 us -> none  [shards(): blocks = jnp.transpose(inverse0.reshape(sr, devices, sr), (1, 0, 2))]
    squeeze x1 -> x0, local copies, waits for them, and re-layouts: 0.75 us -> none  [shards(): w3 = jnp.concatenate([coupling2.T, inverse3, turned[:, 3]], 1)]
where the time goes in v2:
time: 57.4 us; the launch traced here: 57 us
  Pallas kernels  45.6 us (79%)
  local copies, waits for them, and re-layouts  10.7 us (19%)
  between operations  0.64 us (1%)
    pallas_call x1, Pallas kernels, shards(): pl.pallas_call(functools.partial(kernel, devices, front, sr, sizes, cap,...  45.6 us
    unnamed x6, local copies, waits for them, and re-layouts  9.13 us
    pallas_call x1, local copies, waits for them, and re-layouts, shards(): pl.pallas_call(functools.partial(kernel, devices, front, sr, sizes, cap,...  1.61 us

profile of v2, /device:TPU:0, one launch (start us, length us, event | category | flops | bytes accessed | tf_op | source)
XLA Modules:
  0.0 57.0 jit_solution(7089832701455181138)
XLA Ops:
  0.6 1.4 %copy.19.coup2 = f32[128,16]{1,0:T(8,128)} copy(f32[128,16]{0,1:T(8,128)} %param.21) | data formatting | bytes 16384 | tf_op args[8]
  2.1 1.5 %copy.15.owner = s32[256,1]{1,0:T(8,128)} copy(s32[256,1]{0,1:T(1,128)} %param.14) | data formatting | bytes 2048 | tf_op args[1]
  3.5 1.5 %copy.16.sep = f32[4,64,16]{2,1,0:T(8,128)} copy(f32[4,64,16]{1,2,0:T(8,128)} %param.16) | data formatting | bytes 32768 | tf_op args[3]
  5.0 1.5 %copy.18.coup1 = f32[256,16]{1,0:T(8,128)} copy(f32[256,16]{0,1:T(8,128)} %param.20) | data formatting | bytes 32768 | tf_op args[7]
  6.5 1.6 %copy.17.coup0 = f32[512,16]{1,0:T(8,128)} copy(f32[512,16]{0,1:T(8,128)} %param.19) | data formatting | bytes 65536 | tf_op args[6]
  8.1 45.6 %shard_map.140 = (f32[64,1024]{1,0:T(8,128)}, f32[4,64,16]{2,1,0:T(8,128)}) custom-call(f32[64,256]{1,0:T(8,128)} %vals.1, s32[256,1]{1,0:T(8,128)} %copy.15.owner, s32[1,256]{1,0:T(1,128)} %bitcast.1, f32[4,64,16]{2,1,0:T(8,128)} %copy.16.sep, f32[16,512]{1,0:T(8,128)} %inv0.1, f32[16,256]{1,0:T(8,128)} %inv1_own.1, f32[16,128]{1,0:T(8,128)} %inv2_own.1, ...), custom_call_target="tpu_custom_call" | custom-call | tf_op jit(solution)/shard_map/pallas_call | solution.py:394
  53.7 1.6 %copy.20 = f32[4,64,16]{1,2,0:T(8,128)} copy(f32[4,64,16]{2,1,0:T(8,128)} %get-tuple-element.3) | data formatting | bytes 32768 | tf_op jit(solution)/shard_map/pallas_call | solution.py:394
  55.3 1.7 %copy.22 = f32[64,1024]{1,0:T(8,128)} copy(f32[64,1024]{1,0:T(8,128)} %get-tuple-element.6) | data formatting | bytes 524288

commit v3 on v2

--- a/solution.py
+++ b/solution.py
@@ -78,8 +78,7 @@
 
     lax.fori_loop(1, devices, greet, 0)
 
-    eye = iota((elems, elems), 0) == iota((elems, elems), 1)
-    own = jnp.sum(jnp.where(eye, owner[...], 0), axis=0, keepdims=True)
+    own = owner[...]
     marks = iota((devices, elems), 0) == own
     marks_f = jnp.where(marks, 1.0, 0.0).astype(F32)
     earlier = jnp.where(iota((elems, elems), 0) < iota((elems, elems), 1), 1.0, 0.0).astype(BF16)
@@ -107,10 +106,9 @@
         + raw((marks_f * lower).astype(BF16), ranks, NT)
     ).reshape(sendi.shape)
     g1[me % m1] = jnp.concatenate(
-        [jnp.transpose(coup0[...]), inv1_own[...], jnp.transpose(sep[0]), jnp.transpose(sep[1])], 1)
-    own2 = jnp.transpose(sep[2])
-    g2[me % m2] = jnp.concatenate([jnp.transpose(coup1[...]), inv2_own[...], own2, own2], 1)
-    g3[me % m3] = jnp.concatenate([jnp.transpose(coup2[...]), inv3_own[...], jnp.transpose(sep[3])], 1)
+        [coup0[...], inv1_own[...], sep[0], sep[1]], 1)
+    g2[me % m2] = jnp.concatenate([coup1[...], inv2_own[...], sep[2], sep[2]], 1)
+    g3[me % m3] = jnp.concatenate([coup2[...], inv3_own[...], sep[3]], 1)
     recvv[me] = sendv[me]
     recvi[me] = sendi[me]
 
@@ -339,15 +337,15 @@
         piece = blocks[:, side * eight:(side + 1) * eight, :].reshape(devices * eight, sr)
         term = mm(full[side * nrhs:(side + 1) * nrhs], piece, NN)
         sol0 = term if sol0 is None else sol0 + term
-    sep_out[0] = sol0
+    sep_out[0] = jnp.transpose(sol0)
     for level, value, size in ((1, sol1, m1), (2, sol2, m2), (3, sol3, m3)):
         width = value.shape[1]
-        chosen = jnp.where(iota((width, sr), 0) == me % size * sr + iota((width, sr), 1), 1.0, 0.0).astype(BF16)
+        chosen = jnp.where(iota((sr, width), 1) == me % size * sr + iota((sr, width), 0), 1.0, 0.0).astype(BF16)
         a = value.astype(BF16)
         left = value - a.astype(F32)
         b = left.astype(BF16)
         c = (left - b.astype(F32)).astype(BF16)
-        sep_out[level] = raw(a, chosen, NN) + raw(b, chosen, NN) + raw(c, chosen, NN)
+        sep_out[level] = raw(chosen, a, NT) + raw(chosen, b, NT) + raw(chosen, c, NT)
 
     def sent(j, _):
         p = (me + j) % devices
@@ -391,11 +389,11 @@
     vmem = pl.BlockSpec(memory_space=pltpu.VMEM)
     dma = pltpu.SemaphoreType.DMA
     V = pltpu.VMEM
-    return tuple(pl.pallas_call(
+    leaf_solution, sep_solution = pl.pallas_call(
         functools.partial(kernel, devices, front, sr, sizes, cap, half),
         out_shape=(
             jax.ShapeDtypeStruct((nrhs, leaf), F32),
-            jax.ShapeDtypeStruct(sep_loads.shape, F32),
+            jax.ShapeDtypeStruct((sep_loads.shape[0], sr, nrhs), F32),
         ),
         in_specs=[vmem] * 11 + [pl.BlockSpec(memory_space=pl.ANY), vmem],
         out_specs=(vmem, vmem),
@@ -416,9 +414,10 @@
         ],
         compiler_params=pltpu.CompilerParams(
             collective_id=0, has_side_effects=True, vmem_limit_bytes=60 * 1024 * 1024),
-    )(elem_loads, elem_owner, elem_row.reshape(1, elems), sep_loads,
-      inverse0, inverse1, inverse2, inverse3, coupling0, coupling1, coupling2,
-      leaf_inverse, leaf_coupling))
+    )(elem_loads, elem_owner.T, elem_row.reshape(1, elems), jnp.swapaxes(sep_loads, 1, 2),
+      inverse0, inverse1, inverse2, inverse3, coupling0.T, coupling1.T, coupling2.T,
+      leaf_inverse, leaf_coupling)
+    return leaf_solution, jnp.swapaxes(sep_solution, 1, 2)
 
 
 def solution(mesh):

time: 57.4 us -> 49.4 us (0.86)
  local copies, waits for them, and re-layouts: 10.7 us -> 3.05 us
    unnamed x6 -> x2, local copies, waits for them, and re-layouts: 9.13 us -> 3.05 us
    pallas_call x1 -> x0, local copies, waits for them, and re-layouts: 1.61 us -> none  [shards(): pl.pallas_call(functools.partial(kernel, devices, front, sr, sizes, cap,...]
where the time goes in v3:
time: 49.4 us; the launch traced here: 49.1 us
  Pallas kernels  45.4 us (92%)
  local copies, waits for them, and re-layouts  3.05 us (6%)
  between operations  0.64 us (1%)
    pallas_call x1, Pallas kernels, shards(): pl.pallas_call(functools.partial(kernel, devices, front, sr, sizes, cap,...  45.4 us
    unnamed x2, local copies, waits for them, and re-layouts  3.05 us

profile of v3, /device:TPU:0, one launch (start us, length us, event | category | flops | bytes accessed | tf_op | source)
XLA Modules:
  0.0 49.1 jit_solution(5512426171089916517)
XLA Ops:
  0.6 45.4 %shard_map.140 = (f32[64,1024]{1,0:T(8,128)}, f32[4,16,64]{2,1,0:T(8,128)}) custom-call(f32[64,256]{1,0:T(8,128)} %vals.1, s32[1,256]{1,0:T(1,128)} %bitcast.12, s32[1,256]{1,0:T(1,128)} %bitcast.13, f32[4,16,64]{2,1,0:T(8,128)} %bitcast.7, f32[16,512]{1,0:T(8,128)} %inv0.1, f32[16,256]{1,0:T(8,128)} %inv1_own.1, f32[16,128]{1,0:T(8,128)} %inv2_own.1, ...), custom_call_target="tpu_custom_call" | custom-call | tf_op jit(solution)/shard_map/pallas_call | solution.py:392
  46.1 1.7 %copy.17 = f32[64,1024]{1,0:T(8,128)} copy(f32[64,1024]{1,0:T(8,128)} %get-tuple-element.8) | data formatting | bytes 524288
  47.8 1.4 %copy.18 = f32[4,64,16]{1,2,0:T(8,128)} copy(f32[4,64,16]{1,2,0:T(8,128)} %bitcast.9) | data formatting | bytes 32768

commit v4 on v3

--- a/solution.py
+++ b/solution.py
@@ -239,32 +239,39 @@
     group(x3.at[me % m3], x3, x3ss, x3r, m3, "start")
 
     group(g3.at[me % m3], g3, g3s, g3r, m3, "recv")
-    group(g2.at[me % m2], g2, g2s, g2r, m2, "recv")
     c2t = g3[:, :, :n2].reshape(m3 * sr, n2)
     inv3 = g3[:, :, n2:n2 + n3].reshape(m3 * sr, n3)
+    inv3_s = split(inv3)
     s3 = jnp.transpose(g3[:, :, n2 + n3:].reshape(m3 * sr, nrhs))
+    j3 = mm(jnp.transpose(inv3), c2t, NN)
+    j3_s = split(j3)
+    group(g2.at[me % m2], g2, g2s, g2r, m2, "recv")
     c1t = g2[:, :, :n1].reshape(m2 * sr, n1)
     inv2 = g2[:, :, n1:n1 + n2].reshape(m2 * sr, n2)
     s2 = jnp.transpose(g2[:, :, n1 + n2:n1 + n2 + nrhs].reshape(m2 * sr, nrhs))
 
-
     def get_x3(j, _):
         p = me // m3 * m3 + (me + j) % m3
         remote(x3.at[me % m3], x3.at[p % m3], x3ss.at[p % m3], x3r.at[p % m3], p).wait_recv()
         return 0
 
     lax.fori_loop(1, m3, get_x3, 0)
-    y3 = mm(s3 - jnp.sum(x3[...], axis=0), inv3, NT)
-    t2 = mm(y3, c2t, NN)
+    r3 = s3 - jnp.sum(x3[...], axis=0)
+    t2 = mm_split(r3, *j3_s, NN)
     x2s[...] = t2
     copy2 = remote(x2s, x2, ps.at[1], pr.at[1], partner(m3))
     copy2.start()
 
+    j2 = mm(jnp.transpose(inv2), c1t, NN)
+    j2_s = split(j2)
+    r2_base = s2 - t2
+    y3 = mm_split(r3, *inv3_s, NT)
+    q3 = mm_split(y3, *inv3_s, NN)
     wide(g1, g1s, g1r, g1f, "pass")
 
     copy2.wait_recv()
-    y2 = mm(s2 - t2 - x2[...], inv2, NT)
-    t1 = mm(y2, c1t, NN)
+    r2 = r2_base - x2[...]
+    t1 = mm_split(r2, *j2_s, NN)
     x1s[...] = t1
     copy1 = remote(x1s, x1, ps.at[2], pr.at[2], partner(m2))
     copy1.start()
@@ -273,23 +280,26 @@
     inv0_copy.wait_recv()
     c0t = g1[:, :, :n0].reshape(m1 * sr, n0)
     pair0 = jnp.concatenate([inv0[...], inv0_other[...]], 0)
-    hmat = mm(pair0, c0t, NT)
-    hg[me % m1] = hmat
+    inv1_s = split(g1[:, :, n0:n0 + n1].reshape(m1 * sr, n1))
+    k1 = mm_split(mm(pair0, c0t, NT), *inv1_s, NN)
+    hg[me % m1] = k1
     wide(hg, hss, hsr, hf, "start")
-    inv1 = g1[:, :, n0:n0 + n1].reshape(m1 * sr, n1)
     s01 = g1[:, :, n0 + n1:].reshape(m1 * sr, 2 * nrhs)
-    s1 = jnp.transpose(s01[:, nrhs:])
+    s1 = jnp.transpose(s01[:, nrhs:]) - t1
     second = me // m1 == 1
     mine0 = jnp.where(second, pair0[:, n1:], pair0[:, :n1])
     base = mm(mine0, s01[:, :nrhs], NN)
 
     copy1.wait_recv()
-    y1 = mm(s1 - t1 - x1[...], inv1, NT)
-    part = base - mm(hmat, y1, NT)
+    r1 = s1 - x1[...]
+    part = base - mm(k1, r1, NT)
     eight = sr // 2
     x0s[...] = jnp.concatenate([part[sr:sr + eight], part[sr + eight:]], 1)
     copy0 = remote(x0s, x0, ps.at[3], pr.at[3], other0)
     copy0.start()
+    inv2_s = split(inv2)
+    q2 = mm_split(mm_split(r2, *inv2_s, NT), *inv2_s, NN)
+    q1 = mm_split(mm_split(r1, *inv1_s, NT), *inv1_s, NN)
     copy0.wait_recv()
     y0[me] = jnp.concatenate([part[:eight], part[eight:sr]], 1) + x0[...]
 
@@ -305,6 +315,18 @@
     lax.fori_loop(1, devices, send_y, 0)
     wide(hg, hss, hsr, hf, "pass")
     lax.fori_loop(1, devices, send_block, 0)
+    swept = mm_split(jnp.concatenate([leaf_y, coup], 0), lhigh[...], llow[...], NN)
+    leaf_base = swept[:nrhs]
+    lift_s = split(swept[nrhs:])
+    j23_s = split(mm(j3, j2, NN))
+    q32 = q3 - mm_split(q2, *j3_s, NT)
+    wide(hg, hss, hsr, hf, "recv")
+    pieces = []
+    for far in range(2):
+        for side in range(2):
+            low = far * sr + side * eight
+            pieces.append(hg[:, low:low + eight, :].reshape(m1 * eight, n1))
+    k1_s = split(jnp.concatenate(pieces, 0))
 
     def get_block(j, _):
         block_copy(j, True).wait_recv()
@@ -315,20 +337,16 @@
         return 0
 
     lax.fori_loop(1, devices, get_y, 0)
-    wide(hg, hss, hsr, hf, "recv")
-
-    z1 = y1
+
+    parts = []
     for far in range(2):
         where_ = (me // m1 + far) % 2 * m1
         turned = jnp.transpose(y0[pl.ds(where_, m1)].reshape(m1 * eight, 2 * nrhs))
-        for side in range(2):
-            piece = hg[:, far * sr + side * eight:far * sr + (side + 1) * eight, :].reshape(m1 * eight, n1)
-            z1 = z1 - mm(turned[side * nrhs:(side + 1) * nrhs], piece, NN)
-
-    sol1 = mm(z1, inv1, NN)
-    sol2 = mm(y2 - mm(sol1, c1t, NT), inv2, NN)
-    sol3 = mm(y3 - mm(sol2, c2t, NT), inv3, NN)
-    leaf_out[...] = mm_split(leaf_y - mm(sol3, coup, NN), lhigh[...], llow[...], NN)
+        parts += [turned[:nrhs], turned[nrhs:]]
+    sol1 = q1 - mm_split(jnp.concatenate(parts, 1), *k1_s, NN)
+    sol3 = q32 + mm_split(sol1, *j23_s, NT)
+    leaf_out[...] = leaf_base - mm_split(sol3, *lift_s, NN)
+    sol2 = q2 - mm_split(sol1, *j2_s, NT)
 
     lax.fori_loop(1, devices, get_block, 0)
     full = jnp.transpose(y0[...].reshape(devices * eight, 2 * nrhs))

time: 49.4 us -> 49 us (level)
  no operation moved by 1% of the time
where the time goes in v4:
time: 49 us; the launch traced here: 48.8 us
  Pallas kernels  45.1 us (92%)
  local copies, waits for them, and re-layouts  3.05 us (6%)
  between operations  0.64 us (1%)
    pallas_call x1, Pallas kernels, shards(): pl.pallas_call(functools.partial(kernel, devices, front, sr, sizes, cap,...  45.1 us
    unnamed x2, local copies, waits for them, and re-layouts  3.05 us

profile of v4, /device:TPU:0, one launch (start us, length us, event | category | flops | bytes accessed | tf_op | source)
XLA Modules:
  0.0 48.8 jit_solution(702789623297310875)
XLA Ops:
  0.6 45.1 %shard_map.140 = (f32[64,1024]{1,0:T(8,128)}, f32[4,16,64]{2,1,0:T(8,128)}) custom-call(f32[64,256]{1,0:T(8,128)} %vals.1, s32[1,256]{1,0:T(1,128)} %bitcast.12, s32[1,256]{1,0:T(1,128)} %bitcast.13, f32[4,16,64]{2,1,0:T(8,128)} %bitcast.7, f32[16,512]{1,0:T(8,128)} %inv0.1, f32[16,256]{1,0:T(8,128)} %inv1_own.1, f32[16,128]{1,0:T(8,128)} %inv2_own.1, ...), custom_call_target="tpu_custom_call" | custom-call | tf_op jit(solution)/shard_map/pallas_call | solution.py:410
  45.7 1.7 %copy.17 = f32[64,1024]{1,0:T(8,128)} copy(f32[64,1024]{1,0:T(8,128)} %get-tuple-element.8) | data formatting | bytes 524288
  47.4 1.4 %copy.18 = f32[4,64,16]{1,2,0:T(8,128)} copy(f32[4,64,16]{1,2,0:T(8,128)} %bitcast.9) | data formatting | bytes 32768
